TPU v7x, 512 devices: a whole 4x8x8 slice. The times are simulated.
512 devices in a mesh: ctx: 32 (over x, z), exp: 16 (over y, core).
Axes of the slice: x: 4, y: 8, z: 8, core: 2. Of those that a mesh axis runs over, the one named last changes fastest.
Arguments:
- tokens: bfloat16 [8192, 2880], P('ctx', 'exp'), may hold values from -6 to 6
- cotangent: bfloat16 [8192, 2880], P('ctx', 'exp'), may hold values from -4 to 4
- expert_indices: int32 [8192, 4], P('ctx'), may hold values from 0 to 127, all different within a row; in each aligned block of 256 rows (0 to 255, 256 to 511, ...) at most 16 rows name the same one
- routing_weights: float32 [8192, 4], P('ctx'), may hold values from 0.2 to 1
- gate_up_weight_blocks: bfloat16 [32, 2, 2880, 2880], P('ctx', None, 'exp'), may hold values from -6 to 6
- gate_up_block_scales: float32 [32, 2, 2880, 90], P('ctx', None, 'exp'), may hold values from 0.01 to 0.1
- down_weight_blocks: bfloat16 [32, 2880, 2880], P('ctx', 'exp'), may hold values from -6 to 6
- down_block_scales: float32 [32, 2880, 90], P('ctx', 'exp'), may hold values from 0.002 to 0.008
- adapter_down_matrix: bfloat16 [32, 2880, 16], P('ctx', 'exp'), may hold values from -0.109375 to 0.109375
- adapter_up_matrix: bfloat16 [32, 16, 2880], P('ctx', None, 'exp'), may hold values from -1.5 to 1.5
Outputs:
- moe_out: bfloat16 [8192, 2880], P('ctx', 'exp')
- left_gradient: float32 [32, 2880, 16], P('ctx', 'exp')
- right_gradient: float32 [32, 16, 2880], P('ctx', None, 'exp')
Inputs may be any that keep to these rules, and one draw needn't show every extreme that they name: `expert_indices`: each row names 4 different experts. Within the 256 rows of one index of ctx no expert is named more than 16 times, a bound that some block reaches.
All inputs are finite; a program needn't handle non-finite values.
Results may differ from a plain program's by a relative error of at most 0.018.
Values may be sent and summed in bfloat16 or wider, within the bound.
No kernel may reach another device: no remote copies, remote signals or barrier semaphores. Data moves between devices by JAX's collectives and lax.ppermute only.
A program may use at most 64 MiB of HBM per device.

v0:
```python
import jax
import jax.numpy as jnp
from jax import lax
from jax.sharding import PartitionSpec as P

CAP = 16


ADAPTER_SCALE = 0.5
GLU_ALPHA = 1.702
CLAMP_LIMIT = 7.0


def slot_table(expert_indices, flight, capacity):
    flat_ids = expert_indices.reshape(-1)
    onehot = (flat_ids[:, None] == jnp.arange(flight, dtype=jnp.int32)[None, :]).astype(jnp.int32)
    before = jnp.cumsum(onehot, axis=0) - onehot
    position = jnp.sum(before * onehot, axis=1)
    is_live = jnp.sum(onehot, axis=1) > 0
    target = jnp.where(is_live, flat_ids * capacity + position, -1)
    return target.reshape(expert_indices.shape)


def slot_sources(target, slot_count):
    flat_target = target.reshape(-1)
    matches = flat_target[None, :] == jnp.arange(slot_count, dtype=jnp.int32)[:, None]
    pair_index = jnp.arange(flat_target.shape[0], dtype=jnp.int32)
    chosen = jnp.sum(jnp.where(matches, pair_index[None, :], 0), axis=1)
    filled = jnp.any(matches, axis=1)
    return (chosen, filled)


def dispatch_rows(tokens, cotangent, routing_weights, chosen, filled, choices):
    token_of = chosen // choices
    weight_of = jnp.where(filled, routing_weights.reshape(-1)[chosen], 0.0)
    row_data = jnp.where(filled[:, None], tokens[token_of], jnp.zeros((), tokens.dtype))
    gradient_rows = (weight_of[:, None] * cotangent[token_of].astype(jnp.float32)).astype(
        jnp.bfloat16
    )
    return (row_data, gradient_rows)


def dequant_gate_up(blocks, scales):
    pair, hidden, width = blocks.shape
    shaped = blocks.astype(jnp.float32).reshape(pair, hidden, width // 32, 32)
    return (shaped * scales[:, :, :, None]).reshape(pair, hidden, width).astype(jnp.bfloat16)


def dequant_down(blocks, scales):
    hidden, width = blocks.shape
    shaped = blocks.astype(jnp.float32).reshape(hidden, width // 32, 32)
    return (shaped * scales[:, :, None]).reshape(hidden, width).astype(jnp.bfloat16)


def on_device(
    tokens,
    cotangent,
    expert_indices,
    routing_weights,
    gate_up_weight_blocks,
    gate_up_block_scales,
    down_weight_blocks,
    down_block_scales,
    adapter_down_matrix,
    adapter_up_matrix,
):
    flight = lax.axis_size("ctx")
    choices = expert_indices.shape[1]
    slot_count = flight * CAP
    target = slot_table(expert_indices, flight, CAP)
    chosen, filled = slot_sources(target, slot_count)
    w_joined = dequant_gate_up(gate_up_weight_blocks[0], gate_up_block_scales[0])
    w_down = dequant_down(down_weight_blocks[0], down_block_scales[0])
    adapter_left = adapter_down_matrix[0]
    adapter_right = adapter_up_matrix[0]
    whole_rows = lax.all_gather(tokens, "exp", axis=1, tiled=True)
    row_data, gradient_rows = dispatch_rows(
        whole_rows, cotangent, routing_weights, chosen, filled, choices
    )
    got_rows, got_grads = (
        lax.all_to_all(row_data, "ctx", split_axis=0, concat_axis=0, tiled=True),
        lax.all_to_all(gradient_rows, "ctx", split_axis=0, concat_axis=0, tiled=True),
    )
    projected = jnp.einsum("sn,cfn->csf", got_rows, w_joined, preferred_element_type=jnp.float32)
    gate_cut = jnp.minimum(projected[0], CLAMP_LIMIT)
    up_cut = jnp.clip(projected[1], -CLAMP_LIMIT, CLAMP_LIMIT)
    activated = ((up_cut + 1.0) * gate_cut * jax.nn.sigmoid(GLU_ALPHA * gate_cut)).astype(
        jnp.bfloat16
    )
    low_term = jnp.dot(activated, adapter_left, preferred_element_type=jnp.float32)
    back_term = lax.dot_general(
        got_grads, adapter_right, (((1,), (1,)), ((), ())), preferred_element_type=jnp.float32
    )
    low_sum, backward_sum = (
        lax.psum(low_term.astype(jnp.bfloat16), "exp").astype(jnp.float32),
        lax.psum(back_term.astype(jnp.bfloat16), "exp").astype(jnp.float32),
    )
    reduced_rank = low_sum.astype(jnp.bfloat16)
    backward_rank = (ADAPTER_SCALE * backward_sum).astype(jnp.bfloat16)
    base_columns = lax.psum_scatter(
        lax.dot_general(
            w_down, activated, (((0,), (1,)), ((), ())), preferred_element_type=jnp.float32
        ).astype(jnp.bfloat16),
        "exp",
        scatter_dimension=0,
        tiled=True,
    ).astype(jnp.float32)
    adapter_columns = lax.dot_general(
        adapter_right, reduced_rank, (((0,), (1,)), ((), ())), preferred_element_type=jnp.float32
    )
    output_columns = (base_columns + ADAPTER_SCALE * adapter_columns).astype(jnp.bfloat16)
    returned = lax.all_to_all(output_columns, "ctx", split_axis=1, concat_axis=1, tiled=True)
    safe_index = jnp.maximum(target, 0).reshape(-1)
    picked = (
        returned[:, safe_index]
        .astype(jnp.float32)
        .reshape(returned.shape[0], target.shape[0], choices)
    )
    scaled = jnp.where(target >= 0, routing_weights, 0.0)
    moe_out = jnp.sum(picked * scaled[None], axis=2).T.astype(jnp.bfloat16)
    right_gradient = ADAPTER_SCALE * lax.dot_general(
        reduced_rank, got_grads, (((0,), (0,)), ((), ())), preferred_element_type=jnp.float32
    )
    left_gradient = lax.dot_general(
        activated, backward_rank, (((0,), (0,)), ((), ())), preferred_element_type=jnp.float32
    )
    return (moe_out, left_gradient[None], right_gradient[None])


def solution(mesh):
    placed = (
        P("ctx", "exp"),
        P("ctx", "exp"),
        P("ctx", None),
        P("ctx", None),
        P("ctx", None, "exp", None),
        P("ctx", None, "exp", None),
        P("ctx", "exp", None),
        P("ctx", "exp", None),
        P("ctx", "exp", None),
        P("ctx", None, "exp"),
    )
    return jax.shard_map(
        on_device,
        mesh=mesh,
        in_specs=placed,
        out_specs=(P("ctx", "exp"), P("ctx", "exp", None), P("ctx", None, "exp")),
        check_vma=False,
    )
```

profile of v0, /device:TPU:89, one launch (start us, length us, event | category | flops | bytes accessed | tf_op | source)
XLA Modules:
  0.0 269.5 jit_solution(16279499914631724605)
XLA Ops:
  9.0 9.0 %reduce-window.6 = s32[32,8,128]{2,1,0:T(8,128)S(1)} reduce-window(s32[32,8,128]{2,1,0:T(8,128)S(1)} %fusion.16, s32[]{:T(128)} %constant.18.clone.1), window={size=1x1x128 pad=0_0x0_0x127_0}, to_apply=%region_1.2 | reduce-window | flops 4161536 | bytes 262148 | tf_op jit(solution)/shard_map/reduce-window
  19.8 2.3 gather_fusion.2
  22.7 2.0 gather_fusion.3
  25.6 12.0 %all-to-all-start.2 = ((bf16[32,16,180]{2,1,0:T(8,128)(2,1)}), bf16[32,16,180]{2,1,0:T(8,128)(2,1)S(1)}, u32[]{:S(2)}, u32[]{:S(2)}) async-start(bf16[32,16,180]{2,1,0:T(8,128)(2,1)} %fusion.6), calls=%async_computation.2 | async-start | bytes 524288 | tf_op jit(solution)/shard_map/all_to_all | solution.py:82
  37.6 17.7 %all-gather.3.cloned.1.call-done = bf16[16,180,256]{2,1,0:T(8,128)(2,1)} async-done(((bf16[1,180,256]{2,1,0:T(8,128)(2,1)}), bf16[16,180,256]{2,1,0:T(8,128)(2,1)}) %all-gather.3.cloned.1.call-update) | async-done | bytes 1474576 | tf_op jit(solution)/shard_map/all_gather | solution.py:76
  55.3 2.3 reshape.280
  58.6 3.7 %gather_fusion = bf16[512,2880]{1,0:T(8,128)(2,1)} fusion(bf16[256,2880]{1,0:T(8,128)(2,1)S(1)} %bitcast.77, s32[1024]{0:T(1024)S(1)} %pad_clamp_fusion.1), kind=kCustom, calls=%fused_computation | custom fusion | bytes 5900288 | tf_op jit(solution)/shard_map/gather | solution.py:36
  62.3 3.8 %broadcast_select_fusion = bf16[32,16,2880]{2,1,0:T(8,128)(2,1)} fusion(bf16[32,16,2880]{2,1,0:T(8,128)(2,1)} %bitcast.79, pred[32,16]{1,0:T(8,128)(4,1)S(1)} %broadcast_in_dim.57), kind=kLoop, calls=%fused_computation.7 | loop fusion | flops 1474560 | bytes 5898752 | tf_op jit(solution)/shard_map/jit(_where)/select_n | solution.py:36
  66.1 9.7 %all-to-all-start = ((bf16[32,16,2880]{2,1,0:T(8,128)(2,1)}), bf16[32,16,2880]{2,1,0:T(8,128)(2,1)}, u32[]{:S(2)}, u32[]{:S(2)}) async-start(bf16[32,16,2880]{2,1,0:T(8,128)(2,1)} %broadcast_select_fusion), calls=%async_computation | async-start | bytes 6029312 | tf_op jit(solution)/shard_map/all_to_all | solution.py:81
  76.0 5.6 %copy.80 = bf16[1,2,180,2880]{2,3,1,0:T(8,128)(2,1)S(1)} copy(bf16[1,2,180,2880]{3,1,2,0:T(2,128)(2,1)} %param.14) | data formatting | bytes 4147200 | tf_op args[4]
  82.6 2.5 copy.78
  85.1 1.6 copy.99
  87.5 1.4 copy.91
  89.0 1.3 broadcast_maximum_fusion
  95.1 3.0 %fusion.2 = bf16[180,90,32]{0,2,1:T(8,128)(2,1)} fusion(bf16[180,90,32]{0,2,1:T(8,128)(2,1)} %bitcast.82, f32[180,90]{0,1:T(8,128)} %bitcast.89), kind=kLoop, calls=%fused_computation.9 | loop fusion | flops 1555200 | bytes 2138400 | tf_op jit(solution)/shard_map/convert_element_type | solution.py:52
  98.2 2.8 %fusion.1 = bf16[2,180,90,32]{1,3,2,0:T(8,128)(2,1)} fusion(bf16[2,180,90,32]{1,3,2,0:T(8,128)(2,1)S(1)} %bitcast.80, f32[2,180,90]{1,2,0:T(8,128)S(1)} %copy.81), kind=kLoop, calls=%fused_computation.5 | loop fusion | flops 3110400 | bytes 4276800 | tf_op jit(solution)/shard_map/convert_element_type | solution.py:46
  101.1 42.7 %all-to-all-done = bf16[32,16,2880]{2,1,0:T(8,128)(2,1)} async-done(((bf16[32,16,2880]{2,1,0:T(8,128)(2,1)}), bf16[32,16,2880]{2,1,0:T(8,128)(2,1)}, u32[]{:S(2)}, u32[]{:S(2)}) %all-to-all-start) | async-done | bytes 2949152 | tf_op jit(solution)/shard_map/all_to_all | solution.py:81
  143.8 4.8 %convolution_bitcast_fusion = f32[2,512,180]{1,2,0:T(8,128)S(1)} fusion(bf16[2,180,2880]{1,2,0:T(8,128)(2,1)} %bitcast.83, bf16[512,2880,1]{1,0,2:T(8,128)(2,1)} %bitcast.15), kind=kOutput, calls=%fused_computation.13 | convolution fusion | flops 1061683200 | bytes 5760000 | tf_op jit(solution)/shard_map/sn,cfn->csf/dot_general | solution.py:84
  149.6 32.5 %fusion = bf16[184,512]{1,0:T(8,128)(2,1)} fusion(bf16[2880,512]{1,0:T(8,128)(2,1)S(1)} %convolution_convert_fusion), kind=kCustom, calls=%all-reduce-scatter | all-reduce-scatter fusion | flops 1507329 | bytes 3139584
  183.0 5.5 %collective-permute-start = (bf16[60,512]{1,0:T(8,128)(2,1)S(1)}, bf16[60,512]{1,0:T(8,128)(2,1)S(1)}, u32[]{:S(2)}, u32[]{:S(2)}) collective-permute-start(bf16[60,512]{1,0:T(8,128)(2,1)S(1)} %slice.28), channel_id=1, source_target_pairs={{0,1},{1,2},{2,3},{3,4},{4,5},{5,6},{6,7},{7,8},{8,9},{9,10},{10,1... | collective-permute-start | bytes 184328
  188.7 45.1 %all-reduce.2 = (bf16[512,16]{0,1:T(8,128)(2,1)S(1)}, bf16[512,16]{0,1:T(8,128)(2,1)S(1)}) all-reduce(bf16[512,16]{0,1:T(8,128)(2,1)S(1)} %convolution_convert_fusion.2, bf16[512,16]{0,1:T(8,128)(2,1)S(1)} %convolution_convert_fusion.1), channel_id=1, replica_groups=mesh['ctx'=32,'exp'=16] {'exp'}, use_global_device_ids=true, to_apply=%region_7.8 | all-reduce | flops 16384 | bytes 65536 | tf_op jit(solution)/shard_map/psum | solution.py:95
  236.0 8.0 %all-to-all-start.1 = ((bf16[180,32,16]{0,2,1:T(8,128)(2,1)}), bf16[180,32,16]{0,2,1:T(8,128)(2,1)S(1)}, u32[]{:S(2)}, u32[]{:S(2)}) async-start(bf16[180,32,16]{0,2,1:T(8,128)(2,1)} %bitcast.21), calls=%async_computation.1 | async-start | bytes 524288 | tf_op jit(solution)/shard_map/all_to_all | solution.py:112
  245.7 11.1 %all-to-all-done.1 = bf16[180,32,16]{0,2,1:T(8,128)(2,1)S(1)} async-done(((bf16[180,32,16]{0,2,1:T(8,128)(2,1)}), bf16[180,32,16]{0,2,1:T(8,128)(2,1)S(1)}, u32[]{:S(2)}, u32[]{:S(2)}) %all-to-all-start.1) | async-done | bytes 184352 | tf_op jit(solution)/shard_map/all_to_all | solution.py:112
  256.8 3.9 %gather_fusion.1 = bf16[1024,180]{1,0:T(8,128)(2,1)S(1)} fusion(bf16[180,512]{0,1:T(8,128)(2,1)S(1)} %bitcast.78, s32[1024]{0:T(1024)S(1)} %broadcast_clamp_fusion), kind=kCustom, calls=%fused_computation.1 | custom fusion | bytes 741376 | tf_op jit(solution)/shard_map/gather | solution.py:115
  (64 shorter events, 20.1 us)
Async XLA Ops:
  7.2 93.8 %copy-start = (bf16[1,16,180]{2,1,0:T(8,128)(2,1)S(1)}, bf16[1,16,180]{2,1,0:T(8,128)(2,1)}, u32[]{:S(2)}) copy-start(bf16[1,16,180]{2,1,0:T(8,128)(2,1)} %param.19) | copy-start | bytes 17284
  7.2 15.4 %copy-start.2 = (bf16[256,180]{0,1:T(8,128)(2,1)S(1)}, bf16[256,180]{0,1:T(8,128)(2,1)}, u32[]{:S(2)}) copy-start(bf16[256,180]{0,1:T(8,128)(2,1)} %param.11) | copy-start | bytes 276484
  7.2 48.1 %all-gather.3.cloned.1.call-start = ((), (), s32[]{:S(2)}) async-start(), calls=%async_computation.3 | async-start | bytes 1601536 | tf_op jit(solution)/shard_map/all_gather | solution.py:76
  25.6 40.6 %all-to-all-start.2 = ((bf16[32,16,180]{2,1,0:T(8,128)(2,1)}), bf16[32,16,180]{2,1,0:T(8,128)(2,1)S(1)}, u32[]{:S(2)}, u32[]{:S(2)}) async-start(bf16[32,16,180]{2,1,0:T(8,128)(2,1)} %fusion.6), calls=%async_computation.2 | async-start | bytes 524288 | tf_op jit(solution)/shard_map/all_to_all | solution.py:82
  66.1 77.6 %all-to-all-start = ((bf16[32,16,2880]{2,1,0:T(8,128)(2,1)}), bf16[32,16,2880]{2,1,0:T(8,128)(2,1)}, u32[]{:S(2)}, u32[]{:S(2)}) async-start(bf16[32,16,2880]{2,1,0:T(8,128)(2,1)} %broadcast_select_fusion), calls=%async_computation | async-start | bytes 6029312 | tf_op jit(solution)/shard_map/all_to_all | solution.py:81
  76.0 13.0 %copy-start.3 = (s32[256,4]{0,1:T(4,128)S(1)}, s32[256,4]{0,1:T(4,128)}, u32[]{:S(2)}) copy-start(s32[256,4]{0,1:T(4,128)} %param.12) | copy-start | bytes 12292
  143.8 4.9 %copy-start.1 = (bf16[180,90,32]{0,2,1:T(8,128)(2,1)S(1)}, bf16[180,90,32]{0,2,1:T(8,128)(2,1)}, u32[]{:S(2)}) copy-start(bf16[180,90,32]{0,2,1:T(8,128)(2,1)} %fusion.2) | copy-start | bytes 3110404
  149.6 38.9 %copy-start.4 = (bf16[1,180,16]{1,2,0:T(8,128)(2,1)S(1)}, bf16[1,180,16]{1,2,0:T(8,128)(2,1)}, u32[]{:S(2)}) copy-start(bf16[1,180,16]{1,2,0:T(8,128)(2,1)} %param.18) | copy-start | bytes 17284
  183.0 50.8 %collective-permute-start = (bf16[60,512]{1,0:T(8,128)(2,1)S(1)}, bf16[60,512]{1,0:T(8,128)(2,1)S(1)}, u32[]{:S(2)}, u32[]{:S(2)}) collective-permute-start(bf16[60,512]{1,0:T(8,128)(2,1)S(1)} %slice.28), channel_id=1, source_target_pairs={{0,1},{1,2},{2,3},{3,4},{4,5},{5,6},{6,7},{7,8},{8,9},{9,10},{10,1... | collective-permute-start | bytes 184328
  236.0 20.8 %all-to-all-start.1 = ((bf16[180,32,16]{0,2,1:T(8,128)(2,1)}), bf16[180,32,16]{0,2,1:T(8,128)(2,1)S(1)}, u32[]{:S(2)}, u32[]{:S(2)}) async-start(bf16[180,32,16]{0,2,1:T(8,128)(2,1)} %bitcast.21), calls=%async_computation.1 | async-start | bytes 524288 | tf_op jit(solution)/shard_map/all_to_all | solution.py:112
Sparse Core Ops, SparseCore 0:
  10.1 45.1 all-gather.2
where the time goes:
time: 271 us; the launch traced here: 269 us
  blocking collectives  77.6 us (29%)
  waiting for transfers between devices  72.2 us (27%)
  local copies, waits for them, and re-layouts  37.6 us (14%)
  starting transfers between devices  35.3 us (13%)
  other arithmetic  24 us (9%)
  between operations  15 us (6%)
  matrix products  7.75 us (3%)
    psum x1, blocking collectives, on_device(): lax.psum(low_term.astype(jnp.bfloat16), 'exp').astype(jnp.float32)  45.1 us
    all_to_all x1, waiting for transfers between devices, on_device(): lax.all_to_all(row_data, 'ctx', split_axis=0, concat_axis=0, tiled=True)  42.7 us
    unnamed x1, blocking collectives  32.5 us
    all_gather x1, waiting for transfers between devices, on_device(): whole_rows = lax.all_gather(tokens, 'exp', axis=1, tiled=True)  17.7 us
    unnamed x21, local copies, waits for them, and re-layouts  17 us
    all_to_all x1, starting transfers between devices, on_device(): lax.all_to_all(gradient_rows, 'ctx', split_axis=0, concat_axis=0, tiled=T...  12 us
    all_to_all x1, waiting for transfers between devices, on_device(): lax.all_to_all(output_columns, 'ctx', split_axis=1, concat_axis=1, tiled=...  11.1 us
    all_to_all x1, starting transfers between devices, on_device(): lax.all_to_all(row_data, 'ctx', split_axis=0, concat_axis=0, tiled=True)  9.69 us
  transfers between devices with their start and end apart: 5, of which 3 were waited for; matrix products, arithmetic and copies ran while one was open for 20% of the time, Pallas kernels for 0%

commit v1 on v0

v1 whole, which is shorter than its diff:
```python
import jax
import jax.numpy as jnp
from jax import lax
from jax.experimental import pallas as pl
from jax.experimental.pallas import tpu as pltpu
from jax.sharding import PartitionSpec as P


CAP = 16
HALF = CAP // 2
ADAPTER_SCALE = 0.5
GLU_ALPHA = 1.702
CLAMP_LIMIT = 7.0
BF = jnp.bfloat16
F32 = jnp.float32


NN = (((1,), (0,)), ((), ()))
NT = (((1,), (1,)), ((), ()))
TN = (((0,), (0,)), ((), ()))

ORDER = (0, 1, -1, -2, 2, 3, -3, -4)


def dot(a, b, dims):
    return lax.dot_general(a, b, dims, preferred_element_type=F32)


def iota(shape, axis):
    return lax.broadcasted_iota(jnp.int32, shape, axis)


def up8(n):
    return -(-n // 8) * 8


def up128(n):
    return -(-n // 128) * 128


def call(body, out_shape, *args, scalars=1, keep=False, local=(), scratch=()):
    smem = pl.BlockSpec(memory_space=pltpu.SMEM)
    vmem = pl.BlockSpec(memory_space=pltpu.VMEM)
    args = [
        pltpu.with_memory_space_constraint(x, pltpu.VMEM) if i in local else x
        for i, x in enumerate(args)
    ]
    return pl.pallas_call(
        body,
        out_shape=[
            pltpu.VMEM(dims, kind) if keep else pltpu.HBM(dims, kind) for dims, kind in out_shape
        ],
        in_specs=[smem if i < scalars else vmem for i in range(len(args))],
        out_specs=[vmem for _ in out_shape],
        scratch_shapes=list(scratch),
        compiler_params=pltpu.CompilerParams(vmem_limit_bytes=24 << 20),
    )(*args)


def route_rows(where, ids, weights, near, far, rows, grads, pick, weigh):
    side = where[1]
    flight = rows.shape[0] // HALF
    count = ids.shape[1]
    both = near.shape[0]
    width = both // 2
    named = jnp.zeros((flight, count), F32)
    weight = jnp.zeros((flight, count), F32)
    for k in range(ids.shape[0]):
        hit = ids[k : k + 1, :] == iota((flight, count), 0)
        named = named + jnp.where(hit, 1.0, 0.0)
        weight = weight + jnp.where(hit, weights[k : k + 1, :], 0.0)
    earlier = jnp.where(iota((count, count), 0) < iota((count, count), 1), 1.0, 0.0).astype(BF)
    before = dot(named.astype(BF), earlier, NN) - (side * HALF).astype(F32)
    slot = iota((flight, HALF, count), 1).astype(F32)
    taken = (before[:, None, :] == slot) & (named[:, None, :] > 0.5)
    chosen = jnp.where(taken, 1.0, 0.0).reshape(flight * HALF, count)
    scaled = jnp.where(taken, weight[:, None, :], 0.0).reshape(flight * HALF, count)
    one = chosen.astype(BF)
    upper = scaled.astype(BF)
    pick[...] = upper
    weigh[...] = (scaled - upper.astype(F32)).astype(BF)
    row, col = iota((both, both), 0), iota((both, both), 1)

    def features(second):
        inside = (col >= width) if second else (col < width)
        at = row + width if second else row
        left = (at == col + side * width) & inside
        right = (at == col + (1 - side) * width) & inside
        left = jnp.where(left, 1.0, 0.0).astype(BF)
        right = jnp.where(right, 1.0, 0.0).astype(BF)
        return (dot(left, near[...], NN) + dot(right, far[...], NN)).astype(BF)

    rows[...] = dot(one, features(False), NT).astype(BF)
    factor = jnp.sum(scaled, axis=1, keepdims=True)
    grads[...] = (factor * dot(one, features(True), NT)).astype(BF)


def prepare(joined, joined_scales, down, down_scales, left, up, out):
    hidden, width = down.shape
    groups = down_scales.shape[1]
    group = width // groups
    parts = len(ORDER)
    piece = width // parts
    rank = left.shape[0]
    pad = out.shape[2]
    spread = jnp.where(
        iota((groups, width), 1) // group == iota((groups, width), 0), 1.0, 0.0
    ).astype(BF)

    def scaled(codes, scales):
        upper = scales.astype(BF)
        lower = (scales - upper.astype(F32)).astype(BF)
        return codes.astype(F32) * (dot(upper, spread, NN) + dot(lower, spread, NN))

    for c in range(2):
        full = scaled(joined[c], joined_scales[c])
        for a in range(parts):
            out[2 * a + c, :hidden, :piece] = full[:, a * piece : (a + 1) * piece].astype(BF)
    full = scaled(down[...], down_scales[...])
    shifted = jnp.where(iota((rank, pad), 1) == iota((rank, pad), 0) + piece, 1.0, 0.0).astype(BF)
    added = dot(left[...], shifted, TN).astype(BF)
    for a in range(parts):
        out[2 * parts + a, :hidden, :] = added
        out[2 * parts + a, :hidden, :piece] = full[:, a * piece : (a + 1) * piece].astype(BF)
    out[3 * parts, :rank, : up.shape[1]] = up[...]


def source(where, q):
    parts = len(ORDER)
    return lax.rem(where[0] + where[2] * ORDER[q] + parts, parts)


def project_into(where, first, near, far, blocks, before, sums):
    hidden, count = sums.shape[3], sums.shape[2]
    piece = blocks[0].shape[1]
    spans = [(x, h * count) for x in blocks for h in range(2)]
    for n, weights in enumerate((near, far)):
        for c in range(2):
            acc = jnp.zeros((count, hidden), F32) if before is None else before[n, c]
            for q, (x, at) in enumerate(spans):
                part = weights[2 * source(where, first + q) + c, :hidden, :piece]
                acc = acc + dot(x[at : at + count, :], part, NT)
            sums[n, c] = acc


def project_four(where, near, far, first, second, sums):
    project_into(where, 0, near, far, (first, second), None, sums)


def project_more(where, near, far, third, before, sums):
    project_into(where, 4, near, far, (third,), before, sums)


def expert(where, near, far, sums, last, grads, act_near, act_far, up, out, wide):
    side = where[1]
    count, hidden = act_near.shape
    piece = last.shape[1]
    parts = len(ORDER)
    rank = up.shape[0]
    half = piece // 2
    tall = out.shape[0] // parts
    pad = out.shape[1]
    acts = []
    for n, (weights, act) in enumerate(((near, act_near), (far, act_far))):
        total = []
        for c in range(2):
            acc = sums[n, c]
            for h in range(2):
                part = weights[2 * source(where, parts - 2 + h) + c, :hidden, :piece]
                acc = acc + dot(last[h * count : (h + 1) * count, :], part, NT)
            total.append(acc)
        gate = jnp.minimum(total[0], CLAMP_LIMIT)
        lift = jnp.clip(total[1], -CLAMP_LIMIT, CLAMP_LIMIT)
        value = ((lift + 1.0) * gate * jax.nn.sigmoid(GLU_ALPHA * gate)).astype(BF)
        act[...] = value
        acts.append(value)
    row, col = iota((half, piece), 0), iota((half, piece), 1)
    here = jnp.where(row + side * half == col, 1.0, 0.0).astype(BF)
    there = jnp.where(row + (1 - side) * half == col, 1.0, 0.0).astype(BF)
    both = dot(near[3 * parts, :rank, :half], here, NN) + dot(far[3 * parts, :rank, :half], there, NN)
    both = both.astype(BF)
    up[...] = both
    back = dot(both, grads[...], NT)
    for a in range(parts):
        total = dot(acts[0], near[2 * parts + a, :hidden, :], NN) + dot(acts[1], far[2 * parts + a, :hidden, :], NN)
        wide[a * tall : a * tall + count, :] = total
        wide[a * tall + count : (a + 1) * tall, :] = jnp.zeros((tall - count, pad), F32)
        wide[a * tall + count : a * tall + count + rank, :count] = back
    out[...] = wide[...].astype(BF)


def finish(total, up, out):
    count, piece = out.shape
    pad = total.shape[1]
    rank = up.shape[0]
    lift = jnp.where(iota((pad, rank), 0) == iota((pad, rank), 1) + piece, 1.0, 0.0).astype(BF)
    low = dot(total[:count, :], lift, NN).astype(BF)
    added = ADAPTER_SCALE * dot(low, up[...], NN)
    out[...] = (total[:count, :piece].astype(F32) + added).astype(BF)


def gradients(where, total, act_near, act_far, grads, left, right, send):
    side = where[1]
    count, piece = grads.shape
    rank, half = left.shape
    back = (ADAPTER_SCALE * total[count : count + rank, :count].astype(F32)).astype(BF)
    left[...] = dot(back, act_near[...], NN)
    product = dot(total[:count, :], grads[...], TN)
    whole = ADAPTER_SCALE * product[piece : piece + rank]
    first, second = whole[:, :half], whole[:, half:]
    right[...] = jnp.where(side == 0, first, second)
    send[...] = jnp.zeros(send.shape, F32)
    send[:rank, :half] = dot(back, act_far[...], NN)
    send[rank:, :half] = jnp.where(side == 0, second, first)


def combine(where, returned, pick, weigh, ranks, mine, send, whole):
    side = where[1]
    half = mine.shape[0]
    whole[...] = dot(returned[...], pick[...], TN) + dot(returned[...], weigh[...], TN)
    first, second = whole[:half, :], whole[half:, :]
    mine[...] = jnp.where(side == 0, first, second)
    send[:half, :] = jnp.where(side == 0, second, first)
    start = send.shape[0] - ranks.shape[0]
    send[start:, :] = ranks[...]


def settle(mine, left, right, got, out, left_out, right_out):
    half = mine.shape[0]
    rank, wide = left.shape
    start = got.shape[0] - 2 * rank
    out[...] = (mine[...] + got[:half, :]).astype(BF)
    left_out[...] = left[...] + got[start : start + rank, :wide]
    right_out[...] = right[...] + got[start + rank :, :wide]


def on_device(
    tokens,
    cotangent,
    expert_indices,
    routing_weights,
    gate_up_weight_blocks,
    gate_up_block_scales,
    down_weight_blocks,
    down_block_scales,
    adapter_down_matrix,
    adapter_up_matrix,
):
    flight = lax.axis_size("ctx")
    peers = lax.axis_size("exp")
    ring = peers // 2
    index = lax.axis_index("exp")
    chip, side = index // 2, index % 2
    sign = 1 - 2 * ((chip + side) % 2)
    where = jnp.stack([chip, side, sign]).astype(jnp.int32)
    swap_pairs = [(i, i ^ 1) for i in range(peers)]

    def swap(x):
        return lax.ppermute(x, "exp", swap_pairs)

    def trade_along(x, step):
        pairs = []
        for y in range(ring):
            for c in range(2):
                way = step if (y + c) % 2 == 0 else -step
                pairs.append((2 * y + c, 2 * ((y + way) % ring) + c))
        return lax.ppermute(x, "exp", pairs)

    width, count = tokens.shape[1], tokens.shape[0]
    slots = flight * HALF
    hidden, _ = down_weight_blocks.shape[1:]
    piece = 2 * width
    rank = adapter_up_matrix.shape[1]
    pad = up128(piece + rank)

    own = jnp.concatenate([tokens.T, cotangent.T], axis=0)
    other = swap(own)
    rows, grads, pick, weigh = call(
        route_rows,
        [((slots, piece), BF)] * 2 + [((slots, count), BF)] * 2,
        where, expert_indices.T, routing_weights.T, own, other,
        local=(3, 4),
    )

    def trade(x):
        x = x.reshape(flight, HALF, piece)
        return lax.all_to_all(x, "ctx", split_axis=0, concat_axis=0, tiled=True).reshape(slots, piece)

    x0 = trade(rows)
    got_grads = trade(grads)

    (near,) = call(
        prepare,
        [((3 * ring + 1, up8(hidden), pad), BF)],
        gate_up_weight_blocks[0],
        gate_up_block_scales[0],
        down_weight_blocks[0],
        down_block_scales[0],
        adapter_down_matrix[0].T,
        adapter_up_matrix[0],
        scalars=0, keep=True,
    )
    far = swap(near)

    x1 = trade_along(x0, 1)
    first = jnp.concatenate([x0, x1], axis=0)
    second = trade_along(first, -1)
    third = trade_along(second, 1)
    last = trade_along(third, -1)
    (sums,) = call(
        project_four, [((2, 2, slots, hidden), F32)], where, near, far, first, second, local=(1, 2)
    )
    (sums,) = call(
        project_more, [((2, 2, slots, hidden), F32)], where, near, far, third, sums, local=(1, 2)
    )
    tall = slots + rank + 4
    act_near, act_far, up, partial = call(
        expert,
        [((slots, hidden), BF)] * 2 + [((rank, piece), BF), ((ring * tall, pad), BF)],
        where, near, far, sums, last, got_grads,
        local=(1, 2, 4),
        scratch=[pltpu.VMEM((ring * tall, pad), F32)],
    )
    groups = [[2 * y + c for y in range(ring)] for c in range(2)]
    total = lax.psum_scatter(
        partial, "exp", scatter_dimension=0, tiled=True, axis_index_groups=groups
    )
    (expert_rows,) = call(finish, [((slots, piece), BF)], total, up, scalars=0, local=(0,))
    returned = trade(expert_rows)
    left, right, ranks = call(
        gradients,
        [((rank, hidden), F32), ((rank, width), F32), ((2 * rank, count), F32)],
        where, total, act_near, act_far, got_grads,
        keep=True, local=(1,),
    )
    mine, send = call(
        combine,
        [((width, count), F32), ((up8(width) + 2 * rank, count), F32)],
        where, returned, pick, weigh, ranks,
        keep=True, local=(1, 4),
        scratch=[pltpu.VMEM((piece, count), F32)],
    )
    got = swap(send)
    moe, left, right = call(
        settle,
        [((width, count), BF), ((rank, hidden), F32), ((rank, width), F32)],
        mine, left, right, got,
        scalars=0, local=(0, 1, 2, 3),
    )
    return (moe.T, left.T[None], right[None])


def solution(mesh):
    placed = (
        P("ctx", "exp"),
        P("ctx", "exp"),
        P("ctx", None),
        P("ctx", None),
        P("ctx", None, "exp", None),
        P("ctx", None, "exp", None),
        P("ctx", "exp", None),
        P("ctx", "exp", None),
        P("ctx", "exp", None),
        P("ctx", None, "exp"),
    )
    return jax.shard_map(
        on_device,
        mesh=mesh,
        in_specs=placed,
        out_specs=(P("ctx", "exp"), P("ctx", "exp", None), P("ctx", None, "exp")),
        check_vma=False,
    )
```

time: 271 us -> 157 us (0.58)
  the two profiles are of different devices: /device:TPU:89 before, /device:TPU:33 now
where the time goes in v1:
time: 157 us; the launch traced here: 156 us
  blocking collectives  44.9 us (29%)
  starting transfers between devices  42.2 us (27%)
  waiting for transfers between devices  33.6 us (21%)
  Pallas kernels  22.9 us (15%)
  local copies, waits for them, and re-layouts  10.1 us (6%)
  between operations  1.69 us (1%)
    pallas_call x9, Pallas kernels, call(): pl.pallas_call(body, out_shape=[pltpu.VMEM(dims, kind) if keep else pltpu...  22.9 us
    unnamed x1, blocking collectives  22.6 us
    all_to_all x1, blocking collectives, trade(): lax.all_to_all(x, 'ctx', split_axis=0, concat_axis=0, tiled=True)  22.3 us
    ppermute x4, waiting for transfers between devices, trade_along(): return lax.ppermute(x, 'exp', pairs)  18.4 us
    ppermute x3, starting transfers between devices, swap(): return lax.ppermute(x, 'exp', swap_pairs)  16.2 us
    all_to_all x2, starting transfers between devices, trade(): lax.all_to_all(x, 'ctx', split_axis=0, concat_axis=0, tiled=True)  15.3 us
    unnamed x47, local copies, waits for them, and re-layouts  10.1 us
    all_to_all x2, waiting for transfers between devices, trade(): lax.all_to_all(x, 'ctx', split_axis=0, concat_axis=0, tiled=True)  8.02 us
  transfers between devices with their start and end apart: 10, of which 7 were waited for; matrix products, arithmetic and copies ran while one was open for 1% of the time, Pallas kernels for 8%

profile of v1, /device:TPU:33, one launch (start us, length us, event | category | flops | bytes accessed | tf_op | source)
XLA Modules:
  0.0 156.2 jit_solution(16964637310693006011)
XLA Ops:
  0.7 1.9 %copy.21 = bf16[1,2,180,2880]{3,2,1,0:T(8,128)(2,1)S(1)} copy(bf16[1,2,180,2880]{3,1,2,0:T(2,128)(2,1)} %param.14) | data formatting | bytes 4147200 | tf_op args[4]
  2.7 2.4 %shard_map.121.near = bf16[25,184,384]{2,1,0:T(8,128)(2,1)S(1)} custom-call(bf16[2,180,2880]{2,1,0:T(8,128)(2,1)S(1)} %bitcast.35, f32[2,180,90]{2,1,0:T(8,128)S(1)} %bitcast.38, bf16[180,2880]{1,0:T(8,128)(2,1)S(1)} %bitcast.36, f32[180,90]{1,0:T(8,128)S(1)} %bitcast.39, bf16[16,180]{1,0:T(8,128)(2,1)S(1)} %bitcast.40, bf16[16,180]{1,0:T(8,128)(2,1)S(1)} %bitcast.41), custom_call_target="tpu_custom_call" | custom-call | tf_op jit(solution)/shard_map/pallas_call | solution.py:48
  5.1 2.6 %collective-permute-start = (bf16[25,184,384]{2,1,0:T(8,128)(2,1)S(1)}, bf16[25,184,384]{2,1,0:T(8,128)(2,1)}, u32[]{:S(2)}, u32[]{:S(2)}) collective-permute-start(bf16[25,184,384]{2,1,0:T(8,128)(2,1)S(1)} %shard_map.121.near), channel_id=1, source_target_pairs={{0,1},{1,0},{2,3},{3,2},{4,5},{5,4},{6,7},{7,6},{8,9},{9,8},{10,11... | collective-permute-start | bytes 10598408 | tf_op jit(solution)/shard_map/ppermute | solution.py:259
  8.4 1.9 %collective-permute-start.1 = (bf16[360,256]{1,0:T(8,128)(2,1)}, bf16[360,256]{1,0:T(8,128)(2,1)}, u32[]{:S(2)}, u32[]{:S(2)}) collective-permute-start(bf16[360,256]{1,0:T(8,128)(2,1)} %pad_maximum_fusion.1.near), channel_id=1, source_target_pairs={{0,1},{1,0},{2,3},{3,2},{4,5},{5,4},{6,7},{7,6},{8,9},{9,8},{10,11... | collective-permute-start | bytes 552968 | tf_op jit(solution)/shard_map/ppermute | solution.py:259
  10.5 3.5 %collective-permute-done.1.far = bf16[360,256]{1,0:T(8,128)(2,1)} collective-permute-done((bf16[360,256]{1,0:T(8,128)(2,1)}, bf16[360,256]{1,0:T(8,128)(2,1)}, u32[]{:S(2)}, u32[]{:S(2)}) %collective-permute-start.1) | collective-permute-done | bytes 184352 | tf_op jit(solution)/shard_map/ppermute | solution.py:259
  13.9 3.2 %shard_map.122 = (bf16[256,360]{1,0:T(8,128)(2,1)}, bf16[256,360]{1,0:T(8,128)(2,1)}, bf16[256,256]{1,0:T(8,128)(2,1)}, bf16[256,256]{1,0:T(8,128)(2,1)}) custom-call(s32[3]{0:T(128)S(1)} %pad_add_fusion.where, s32[4,256]{1,0:T(4,128)S(1)} %bitcast.42, f32[4,256]{1,0:T(4,128)S(1)} %bitcast.43, bf16[360,256]{1,0:T(8,128)(2,1)} %pad_maximum_fusion.1.near, ...), custom_call_target="tpu_custom_call" | custom-call | tf_op jit(solution)/shard_map/pallas_call | solution.py:48
  17.1 22.3 %all_to_all.15 = bf16[32,8,360]{2,1,0:T(8,128)(2,1)S(1)} all-to-all(bf16[32,8,360]{2,1,0:T(8,128)(2,1)} %bitcast.48), channel_id=1, replica_groups=mesh['ctx'=32,'exp'=16] {'ctx'}, dimensions={0} | all-to-all | bytes 368640 | tf_op jit(solution)/shard_map/all_to_all | solution.py:287
  39.4 2.1 %collective-permute-start.2 = (bf16[256,360]{1,0:T(8,128)(2,1)S(1)}, bf16[256,360]{1,0:T(8,128)(2,1)S(1)}, u32[]{:S(2)}, u32[]{:S(2)}) collective-permute-start(bf16[256,360]{1,0:T(8,128)(2,1)S(1)} %bitcast.45), channel_id=1, source_target_pairs={{0,2},{1,15},{2,0},{3,5},{4,6},{5,3},{6,4},{7,9},{8,10},{9,7},{10,... | collective-permute-start | bytes 552968 | tf_op jit(solution)/shard_map/ppermute | solution.py:267
  41.5 5.5 %collective-permute-done.2 = bf16[256,360]{1,0:T(8,128)(2,1)S(1)} collective-permute-done((bf16[256,360]{1,0:T(8,128)(2,1)S(1)}, bf16[256,360]{1,0:T(8,128)(2,1)S(1)}, u32[]{:S(2)}, u32[]{:S(2)}) %collective-permute-start.2) | collective-permute-done | bytes 184352 | tf_op jit(solution)/shard_map/ppermute | solution.py:267
  47.1 1.9 %collective-permute-start.3 = (bf16[512,360]{1,0:T(8,128)(2,1)S(1)}, bf16[512,360]{1,0:T(8,128)(2,1)S(1)}, u32[]{:S(2)}, u32[]{:S(2)}) collective-permute-start(bf16[512,360]{1,0:T(8,128)(2,1)S(1)} %pad_maximum_fusion.first), channel_id=1, source_target_pairs={{0,14},{1,3},{2,4},{3,1},{4,2},{5,7},{6,8},{7,5},{8,6},{9,11},{10,... | collective-permute-start | bytes 1105928 | tf_op jit(solution)/shard_map/ppermute | solution.py:267
  49.8 5.8 %collective-permute-done.3.second = bf16[512,360]{1,0:T(8,128)(2,1)S(1)} collective-permute-done((bf16[512,360]{1,0:T(8,128)(2,1)S(1)}, bf16[512,360]{1,0:T(8,128)(2,1)S(1)}, u32[]{:S(2)}, u32[]{:S(2)}) %collective-permute-start.3) | collective-permute-done | bytes 368672 | tf_op jit(solution)/shard_map/ppermute | solution.py:267
  55.6 2.1 %collective-permute-start.4 = (bf16[512,360]{1,0:T(8,128)(2,1)S(1)}, bf16[512,360]{1,0:T(8,128)(2,1)}, u32[]{:S(2)}, u32[]{:S(2)}) collective-permute-start(bf16[512,360]{1,0:T(8,128)(2,1)S(1)} %collective-permute-done.3.second), channel_id=1, source_target_pairs={{0,2},{1,15},{2,0},{3,5},{4,6},{5,3},{6,4},{7,9},{8,10},{9,7},{10,... | collective-permute-start | bytes 1105928 | tf_op jit(solution)/shard_map/ppermute | solution.py:267
  58.4 7.0 %collective-permute-done.4.third = bf16[512,360]{1,0:T(8,128)(2,1)} collective-permute-done((bf16[512,360]{1,0:T(8,128)(2,1)S(1)}, bf16[512,360]{1,0:T(8,128)(2,1)}, u32[]{:S(2)}, u32[]{:S(2)}) %collective-permute-start.4) | collective-permute-done | bytes 368672 | tf_op jit(solution)/shard_map/ppermute | solution.py:267
  65.4 1.9 %collective-permute-start.5 = (bf16[512,360]{1,0:T(8,128)(2,1)}, bf16[512,360]{1,0:T(8,128)(2,1)}, u32[]{:S(2)}, u32[]{:S(2)}) collective-permute-start(bf16[512,360]{1,0:T(8,128)(2,1)} %collective-permute-done.4.third), channel_id=1, source_target_pairs={{0,14},{1,3},{2,4},{3,1},{4,2},{5,7},{6,8},{7,5},{8,6},{9,11},{10,... | collective-permute-start | bytes 1105928 | tf_op jit(solution)/shard_map/ppermute | solution.py:267
  67.3 5.9 %all-to-all-start.1 = ((bf16[32,8,360]{2,1,0:T(8,128)(2,1)}), bf16[32,8,360]{2,1,0:T(8,128)(2,1)}, u32[]{:S(2)}, u32[]{:S(2)}) async-start(bf16[32,8,360]{2,1,0:T(8,128)(2,1)} %bitcast.47), calls=%async_computation.1 | async-start | bytes 393216 | tf_op jit(solution)/shard_map/all_to_all | solution.py:287
  75.2 4.2 %shard_map.123.before = f32[2,2,256,180]{3,2,1,0:T(8,128)} custom-call(s32[3]{0:T(128)S(1)} %pad_add_fusion.where, bf16[25,184,384]{2,1,0:T(8,128)(2,1)S(1)} %shard_map.121.near, bf16[25,184,384]{2,1,0:T(8,128)(2,1)} %collective-permute-done.far, bf16[512,360]{1,0:T(8,128)(2,1)S(1)} %copy-done.3, bf16[512,360]{1,0:T(8,128)(2,1)S(1)} %copy-done.6), custom_call_target="tpu_custom_call" | custom-call | tf_op jit(solution)/shard_map/pallas_call | solution.py:48
  80.7 3.8 %shard_map.124.sums = f32[2,2,256,180]{3,2,1,0:T(8,128)} custom-call(s32[3]{0:T(128)S(1)} %pad_add_fusion.where, bf16[25,184,384]{2,1,0:T(8,128)(2,1)S(1)} %shard_map.121.near, bf16[25,184,384]{2,1,0:T(8,128)(2,1)} %collective-permute-done.far, bf16[512,360]{1,0:T(8,128)(2,1)} %collective-permute-done.4.third, f32[2,2,256,180]{3,2,1,0:T(8,128)S(1)} %copy-done.1), custom_call_target="tpu_custom_call" | custom-call | tf_op jit(solution)/shard_map/pallas_call | solution.py:48
  85.7 5.4 %shard_map.125 = (bf16[256,180]{1,0:T(8,128)(2,1)}, bf16[256,180]{1,0:T(8,128)(2,1)}, bf16[16,360]{1,0:T(8,128)(2,1)}, bf16[2208,384]{1,0:T(8,128)(2,1)}) custom-call(s32[3]{0:T(128)S(1)} %pad_add_fusion.where, bf16[25,184,384]{2,1,0:T(8,128)(2,1)S(1)} %shard_map.121.near, bf16[25,184,384]{2,1,0:T(8,128)(2,1)} %collective-permute-done.far, ...), custom_call_target="tpu_custom_call" | custom-call | tf_op jit(solution)/shard_map/pallas_call | solution.py:48
  91.1 22.6 %fusion = bf16[288,384]{1,0:T(8,128)(2,1)S(1)} fusion(bf16[2208,384]{1,0:T(8,128)(2,1)} %get-tuple-element.21), kind=kCustom, calls=%all-reduce-scatter | all-reduce-scatter fusion | flops 884737 | bytes 1918976
  113.8 2.8 %collective-permute-start.7 = (bf16[84,384]{1,0:T(8,128)(2,1)S(1)}, bf16[84,384]{1,0:T(8,128)(2,1)S(1)}, u32[]{:S(2)}, u32[]{:S(2)}) collective-permute-start(bf16[84,384]{1,0:T(8,128)(2,1)S(1)} %slice), channel_id=1, source_target_pairs={{0,2},{2,4},{4,6},{6,8},{8,10},{10,12},{12,14},{1,3},{3,5},{5,7},{... | collective-permute-start | bytes 193544
  118.4 2.7 %collective-permute-done.7 = bf16[84,384]{1,0:T(8,128)(2,1)S(1)} collective-permute-done((bf16[84,384]{1,0:T(8,128)(2,1)S(1)}, bf16[84,384]{1,0:T(8,128)(2,1)S(1)}, u32[]{:S(2)}, u32[]{:S(2)}) %collective-permute-start.7) | collective-permute-done | bytes 64544
  123.1 9.4 %all-to-all-start.2 = ((bf16[32,8,360]{2,1,0:T(8,128)(2,1)}), bf16[32,8,360]{2,1,0:T(8,128)(2,1)S(1)}, u32[]{:S(2)}, u32[]{:S(2)}) async-start(bf16[32,8,360]{2,1,0:T(8,128)(2,1)} %bitcast.44), calls=%async_computation.2 | async-start | bytes 393216 | tf_op jit(solution)/shard_map/all_to_all | solution.py:287
  133.9 8.0 %all-to-all-done.2 = bf16[32,8,360]{2,1,0:T(8,128)(2,1)S(1)} async-done(((bf16[32,8,360]{2,1,0:T(8,128)(2,1)}), bf16[32,8,360]{2,1,0:T(8,128)(2,1)S(1)}, u32[]{:S(2)}, u32[]{:S(2)}) %all-to-all-start.2) | async-done | bytes 184352 | tf_op jit(solution)/shard_map/all_to_all | solution.py:287
  142.8 11.7 %collective-permute-start.6 = (f32[216,256]{1,0:T(8,128)S(1)}, f32[216,256]{1,0:T(8,128)S(1)}, u32[]{:S(2)}, u32[]{:S(2)}) collective-permute-start(f32[216,256]{1,0:T(8,128)S(1)} %get-tuple-element.31), channel_id=1, source_target_pairs={{0,1},{1,0},{2,3},{3,2},{4,5},{5,4},{6,7},{7,6},{8,9},{9,8},{10,11... | collective-permute-start | bytes 663560 | tf_op jit(solution)/shard_map/ppermute | solution.py:259
  (57 shorter events, 14.0 us)
Async XLA Ops:
  0.6 2.0 %copy-start.16 = (f32[1,2,180,90]{3,1,2,0:T(2,128)S(1)}, f32[1,2,180,90]{3,1,2,0:T(2,128)}, u32[]{:S(2)}) copy-start(f32[1,2,180,90]{3,1,2,0:T(2,128)} %param.15) | copy-start | bytes 388804
  0.6 2.0 %copy-start.19 = (f32[1,180,90]{2,0,1:T(1,128)S(1)}, f32[1,180,90]{2,0,1:T(1,128)}, u32[]{:S(2)}) copy-start(f32[1,180,90]{2,0,1:T(1,128)} %param.17) | copy-start | bytes 194404
  0.7 2.0 %copy-start.4 = (bf16[1,180,2880]{2,1,0:T(8,128)(2,1)S(1)}, bf16[1,180,2880]{2,1,0:T(8,128)(2,1)}, u32[]{:S(2)}) copy-start(bf16[1,180,2880]{2,1,0:T(8,128)(2,1)} %param.16) | copy-start | bytes 3110404
  0.7 2.0 %copy-start.12 = (bf16[1,180,16]{1,2,0:T(8,128)(2,1)S(1)}, bf16[1,180,16]{1,2,0:T(8,128)(2,1)}, u32[]{:S(2)}) copy-start(bf16[1,180,16]{1,2,0:T(8,128)(2,1)} %param.18) | copy-start | bytes 17284
  0.7 2.0 %copy-start.13 = (bf16[1,16,180]{2,1,0:T(8,128)(2,1)S(1)}, bf16[1,16,180]{2,1,0:T(8,128)(2,1)}, u32[]{:S(2)}) copy-start(bf16[1,16,180]{2,1,0:T(8,128)(2,1)} %param.19) | copy-start | bytes 17284
  2.7 5.0 %copy-start.17 = (bf16[256,180]{0,1:T(8,128)(2,1)S(1)}, bf16[256,180]{0,1:T(8,128)(2,1)}, u32[]{:S(2)}) copy-start(bf16[256,180]{0,1:T(8,128)(2,1)} %param.11) | copy-start | bytes 276484
  2.7 5.0 %copy-start.18 = (bf16[256,180]{0,1:T(8,128)(2,1)S(1)}, bf16[256,180]{0,1:T(8,128)(2,1)}, u32[]{:S(2)}) copy-start(bf16[256,180]{0,1:T(8,128)(2,1)} %param.10) | copy-start | bytes 276484
  2.7 11.2 %copy-start.14 = (s32[256,4]{0,1:T(4,128)S(1)}, s32[256,4]{0,1:T(4,128)}, u32[]{:S(2)}) copy-start(s32[256,4]{0,1:T(4,128)} %param.12) | copy-start | bytes 12292
  2.7 11.2 %copy-start.15 = (f32[256,4]{0,1:T(4,128)S(1)}, f32[256,4]{0,1:T(4,128)}, u32[]{:S(2)}) copy-start(f32[256,4]{0,1:T(4,128)} %param.13) | copy-start | bytes 12292
  5.1 68.1 %collective-permute-start = (bf16[25,184,384]{2,1,0:T(8,128)(2,1)S(1)}, bf16[25,184,384]{2,1,0:T(8,128)(2,1)}, u32[]{:S(2)}, u32[]{:S(2)}) collective-permute-start(bf16[25,184,384]{2,1,0:T(8,128)(2,1)S(1)} %shard_map.121.near), channel_id=1, source_target_pairs={{0,1},{1,0},{2,3},{3,2},{4,5},{5,4},{6,7},{7,6},{8,9},{9,8},{10,11... | collective-permute-start | bytes 10598408 | tf_op jit(solution)/shard_map/ppermute | solution.py:259
  8.4 5.5 %collective-permute-start.1 = (bf16[360,256]{1,0:T(8,128)(2,1)}, bf16[360,256]{1,0:T(8,128)(2,1)}, u32[]{:S(2)}, u32[]{:S(2)}) collective-permute-start(bf16[360,256]{1,0:T(8,128)(2,1)} %pad_maximum_fusion.1.near), channel_id=1, source_target_pairs={{0,1},{1,0},{2,3},{3,2},{4,5},{5,4},{6,7},{7,6},{8,9},{9,8},{10,11... | collective-permute-start | bytes 552968 | tf_op jit(solution)/shard_map/ppermute | solution.py:259
  39.4 7.6 %collective-permute-start.2 = (bf16[256,360]{1,0:T(8,128)(2,1)S(1)}, bf16[256,360]{1,0:T(8,128)(2,1)S(1)}, u32[]{:S(2)}, u32[]{:S(2)}) collective-permute-start(bf16[256,360]{1,0:T(8,128)(2,1)S(1)} %bitcast.45), channel_id=1, source_target_pairs={{0,2},{1,15},{2,0},{3,5},{4,6},{5,3},{6,4},{7,9},{8,10},{9,7},{10,... | collective-permute-start | bytes 552968 | tf_op jit(solution)/shard_map/ppermute | solution.py:267
  47.1 8.5 %collective-permute-start.3 = (bf16[512,360]{1,0:T(8,128)(2,1)S(1)}, bf16[512,360]{1,0:T(8,128)(2,1)S(1)}, u32[]{:S(2)}, u32[]{:S(2)}) collective-permute-start(bf16[512,360]{1,0:T(8,128)(2,1)S(1)} %pad_maximum_fusion.first), channel_id=1, source_target_pairs={{0,14},{1,3},{2,4},{3,1},{4,2},{5,7},{6,8},{7,5},{8,6},{9,11},{10,... | collective-permute-start | bytes 1105928 | tf_op jit(solution)/shard_map/ppermute | solution.py:267
  55.6 9.8 %collective-permute-start.4 = (bf16[512,360]{1,0:T(8,128)(2,1)S(1)}, bf16[512,360]{1,0:T(8,128)(2,1)}, u32[]{:S(2)}, u32[]{:S(2)}) collective-permute-start(bf16[512,360]{1,0:T(8,128)(2,1)S(1)} %collective-permute-done.3.second), channel_id=1, source_target_pairs={{0,2},{1,15},{2,0},{3,5},{4,6},{5,3},{6,4},{7,9},{8,10},{9,7},{10,... | collective-permute-start | bytes 1105928 | tf_op jit(solution)/shard_map/ppermute | solution.py:267
  65.4 19.1 %collective-permute-start.5 = (bf16[512,360]{1,0:T(8,128)(2,1)}, bf16[512,360]{1,0:T(8,128)(2,1)}, u32[]{:S(2)}, u32[]{:S(2)}) collective-permute-start(bf16[512,360]{1,0:T(8,128)(2,1)} %collective-permute-done.4.third), channel_id=1, source_target_pairs={{0,14},{1,3},{2,4},{3,1},{4,2},{5,7},{6,8},{7,5},{8,6},{9,11},{10,... | collective-permute-start | bytes 1105928 | tf_op jit(solution)/shard_map/ppermute | solution.py:267
  67.3 17.2 %all-to-all-start.1 = ((bf16[32,8,360]{2,1,0:T(8,128)(2,1)}), bf16[32,8,360]{2,1,0:T(8,128)(2,1)}, u32[]{:S(2)}, u32[]{:S(2)}) async-start(bf16[32,8,360]{2,1,0:T(8,128)(2,1)} %bitcast.47), calls=%async_computation.1 | async-start | bytes 393216 | tf_op jit(solution)/shard_map/all_to_all | solution.py:287
  91.1 30.9 %copy-start.11 = (bf16[16,360]{1,0:T(8,128)(2,1)S(1)}, bf16[16,360]{1,0:T(8,128)(2,1)}, u32[]{:S(2)}) copy-start(bf16[16,360]{1,0:T(8,128)(2,1)} %get-tuple-element.22.up) | copy-start | bytes 34564
  91.1 41.4 %copy-start.9 = (bf16[256,180]{1,0:T(8,128)(2,1)S(1)}, bf16[256,180]{1,0:T(8,128)(2,1)}, u32[]{:S(2)}) copy-start(bf16[256,180]{1,0:T(8,128)(2,1)} %get-tuple-element.25.act_near) | copy-start | bytes 276484
  91.1 41.4 %copy-start.10 = (bf16[256,180]{1,0:T(8,128)(2,1)S(1)}, bf16[256,180]{1,0:T(8,128)(2,1)}, u32[]{:S(2)}) copy-start(bf16[256,180]{1,0:T(8,128)(2,1)} %get-tuple-element.26.act_far) | copy-start | bytes 276484
  113.7 28.2 %copy-start.7 = (bf16[256,256]{1,0:T(8,128)(2,1)S(1)}, bf16[256,256]{1,0:T(8,128)(2,1)}, u32[]{:S(2)}) copy-start(bf16[256,256]{1,0:T(8,128)(2,1)} %get-tuple-element.23.pick) | copy-start | bytes 393220
  113.7 28.2 %copy-start.8 = (bf16[256,256]{1,0:T(8,128)(2,1)S(1)}, bf16[256,256]{1,0:T(8,128)(2,1)}, u32[]{:S(2)}) copy-start(bf16[256,256]{1,0:T(8,128)(2,1)} %get-tuple-element.24.weigh) | copy-start | bytes 393220
  113.8 7.3 %collective-permute-start.7 = (bf16[84,384]{1,0:T(8,128)(2,1)S(1)}, bf16[84,384]{1,0:T(8,128)(2,1)S(1)}, u32[]{:S(2)}, u32[]{:S(2)}) collective-permute-start(bf16[84,384]{1,0:T(8,128)(2,1)S(1)} %slice), channel_id=1, source_target_pairs={{0,2},{2,4},{4,6},{6,8},{8,10},{10,12},{12,14},{1,3},{3,5},{5,7},{... | collective-permute-start | bytes 193544
  123.1 18.8 %all-to-all-start.2 = ((bf16[32,8,360]{2,1,0:T(8,128)(2,1)}), bf16[32,8,360]{2,1,0:T(8,128)(2,1)S(1)}, u32[]{:S(2)}, u32[]{:S(2)}) async-start(bf16[32,8,360]{2,1,0:T(8,128)(2,1)} %bitcast.44), calls=%async_computation.2 | async-start | bytes 393216 | tf_op jit(solution)/shard_map/all_to_all | solution.py:287
  142.8 12.8 %collective-permute-start.6 = (f32[216,256]{1,0:T(8,128)S(1)}, f32[216,256]{1,0:T(8,128)S(1)}, u32[]{:S(2)}, u32[]{:S(2)}) collective-permute-start(f32[216,256]{1,0:T(8,128)S(1)} %get-tuple-element.31), channel_id=1, source_target_pairs={{0,1},{1,0},{2,3},{3,2},{4,5},{5,4},{6,7},{7,6},{8,9},{9,8},{10,11... | collective-permute-start | bytes 663560 | tf_op jit(solution)/shard_map/ppermute | solution.py:259
  (6 other events, 5.9 us)

commit v2 on v1

--- a/solution.py
+++ b/solution.py
@@ -38,11 +38,13 @@
     return -(-n // 128) * 128
 
 
-def call(body, out_shape, *args, scalars=1, keep=False, local=(), scratch=()):
+def call(body, out_shape, *args, scalars=1, keep=False, local=(), free=(), scratch=()):
     smem = pl.BlockSpec(memory_space=pltpu.SMEM)
     vmem = pl.BlockSpec(memory_space=pltpu.VMEM)
     args = [
-        pltpu.with_memory_space_constraint(x, pltpu.VMEM) if i in local else x
+        x
+        if i < scalars or i in free
+        else pltpu.with_memory_space_constraint(x, pltpu.VMEM if i in local else pltpu.HBM)
         for i, x in enumerate(args)
     ]
     return pl.pallas_call(
@@ -57,12 +59,10 @@
     )(*args)
 
 
-def route_rows(where, ids, weights, near, far, rows, grads, pick, weigh):
-    side = where[1]
-    flight = rows.shape[0] // HALF
-    count = ids.shape[1]
-    both = near.shape[0]
-    width = both // 2
+def assign(where, ids, weights, pick, weigh, one):
+    side = where[1]
+    slots, count = pick.shape
+    flight = slots // HALF
     named = jnp.zeros((flight, count), F32)
     weight = jnp.zeros((flight, count), F32)
     for k in range(ids.shape[0]):
@@ -73,31 +73,40 @@
     before = dot(named.astype(BF), earlier, NN) - (side * HALF).astype(F32)
     slot = iota((flight, HALF, count), 1).astype(F32)
     taken = (before[:, None, :] == slot) & (named[:, None, :] > 0.5)
-    chosen = jnp.where(taken, 1.0, 0.0).reshape(flight * HALF, count)
-    scaled = jnp.where(taken, weight[:, None, :], 0.0).reshape(flight * HALF, count)
-    one = chosen.astype(BF)
+    one[...] = jnp.where(taken, 1.0, 0.0).reshape(slots, count).astype(BF)
+    scaled = jnp.where(taken, weight[:, None, :], 0.0).reshape(slots, count)
     upper = scaled.astype(BF)
     pick[...] = upper
     weigh[...] = (scaled - upper.astype(F32)).astype(BF)
-    row, col = iota((both, both), 0), iota((both, both), 1)
-
-    def features(second):
-        inside = (col >= width) if second else (col < width)
-        at = row + width if second else row
-        left = (at == col + side * width) & inside
-        right = (at == col + (1 - side) * width) & inside
-        left = jnp.where(left, 1.0, 0.0).astype(BF)
-        right = jnp.where(right, 1.0, 0.0).astype(BF)
-        return (dot(left, near[...], NN) + dot(right, far[...], NN)).astype(BF)
-
-    rows[...] = dot(one, features(False), NT).astype(BF)
-    factor = jnp.sum(scaled, axis=1, keepdims=True)
-    grads[...] = (factor * dot(one, features(True), NT)).astype(BF)
+
+
+def features(where, near, far):
+    side = where[1]
+    width = near.shape[0]
+    row, col = iota((2 * width, width), 0), iota((2 * width, width), 1)
+    left = jnp.where(row == col + side * width, 1.0, 0.0).astype(BF)
+    right = jnp.where(row == col + (1 - side) * width, 1.0, 0.0).astype(BF)
+    return (dot(left, near[...], NN) + dot(right, far[...], NN)).astype(BF)
+
+
+def select_rows(where, one, near, far, rows):
+    rows[...] = dot(one[...], features(where, near, far), NT).astype(BF)
+
+
+def select_grads(where, one, pick, weigh, near, far, grads):
+    factor = jnp.sum(pick[...].astype(F32) + weigh[...].astype(F32), axis=1, keepdims=True)
+    grads[...] = (factor * dot(one[...], features(where, near, far), NT)).astype(BF)
+
+
+def join(first, second, out):
+    count = first.shape[0]
+    out[:count, :] = first[...]
+    out[count:, :] = second[...]
 
 
 def prepare(joined, joined_scales, down, down_scales, left, up, out):
     hidden, width = down.shape
-    groups = down_scales.shape[1]
+    groups = down_scales.shape[2]
     group = width // groups
     parts = len(ORDER)
     piece = width // parts
@@ -113,10 +122,10 @@
         return codes.astype(F32) * (dot(upper, spread, NN) + dot(lower, spread, NN))
 
     for c in range(2):
-        full = scaled(joined[c], joined_scales[c])
+        full = scaled(joined[:, c, :], joined_scales[:, c, :])
         for a in range(parts):
             out[2 * a + c, :hidden, :piece] = full[:, a * piece : (a + 1) * piece].astype(BF)
-    full = scaled(down[...], down_scales[...])
+    full = scaled(down[...], down_scales[:, 0, :])
     shifted = jnp.where(iota((rank, pad), 1) == iota((rank, pad), 0) + piece, 1.0, 0.0).astype(BF)
     added = dot(left[...], shifted, TN).astype(BF)
     for a in range(parts):
@@ -273,13 +282,16 @@
     rank = adapter_up_matrix.shape[1]
     pad = up128(piece + rank)
 
-    own = jnp.concatenate([tokens.T, cotangent.T], axis=0)
-    other = swap(own)
-    rows, grads, pick, weigh = call(
-        route_rows,
-        [((slots, piece), BF)] * 2 + [((slots, count), BF)] * 2,
-        where, expert_indices.T, routing_weights.T, own, other,
-        local=(3, 4),
+    tok, cot = tokens.T, cotangent.T
+    tok_far = swap(tok)
+    cot_far = swap(cot)
+    pick, weigh, one = call(
+        assign, [((slots, count), BF)] * 3, where, expert_indices.T, routing_weights.T,
+    )
+    (rows,) = call(select_rows, [((slots, piece), BF)], where, one, tok, tok_far, local=(3,))
+    (grads,) = call(
+        select_grads, [((slots, piece), BF)], where, one, pick, weigh, cot, cot_far,
+        local=(5,),
     )
 
     def trade(x):
@@ -292,10 +304,10 @@
     (near,) = call(
         prepare,
         [((3 * ring + 1, up8(hidden), pad), BF)],
-        gate_up_weight_blocks[0],
-        gate_up_block_scales[0],
+        gate_up_weight_blocks[0].transpose(1, 0, 2),
+        gate_up_block_scales[0].transpose(1, 0, 2),
         down_weight_blocks[0],
-        down_block_scales[0],
+        down_block_scales[0][:, None, :],
         adapter_down_matrix[0].T,
         adapter_up_matrix[0],
         scalars=0, keep=True,
@@ -303,12 +315,12 @@
     far = swap(near)
 
     x1 = trade_along(x0, 1)
-    first = jnp.concatenate([x0, x1], axis=0)
+    (first,) = call(join, [((2 * slots, piece), BF)], x0, x1, scalars=0, keep=True, local=(1,))
     second = trade_along(first, -1)
     third = trade_along(second, 1)
     last = trade_along(third, -1)
     (sums,) = call(
-        project_four, [((2, 2, slots, hidden), F32)], where, near, far, first, second, local=(1, 2)
+        project_four, [((2, 2, slots, hidden), F32)], where, near, far, first, second, local=(1, 2, 3)
     )
     (sums,) = call(
         project_more, [((2, 2, slots, hidden), F32)], where, near, far, third, sums, local=(1, 2)
@@ -325,7 +337,7 @@
     total = lax.psum_scatter(
         partial, "exp", scatter_dimension=0, tiled=True, axis_index_groups=groups
     )
-    (expert_rows,) = call(finish, [((slots, piece), BF)], total, up, scalars=0, local=(0,))
+    (expert_rows,) = call(finish, [((slots, piece), BF)], total, up, scalars=0, local=(0,), free=(1,))
     returned = trade(expert_rows)
     left, right, ranks = call(
         gradients,
@@ -337,7 +349,7 @@
         combine,
         [((width, count), F32), ((up8(width) + 2 * rank, count), F32)],
         where, returned, pick, weigh, ranks,
-        keep=True, local=(1, 4),
+        keep=True, local=(1, 4), free=(2, 3),
         scratch=[pltpu.VMEM((piece, count), F32)],
     )
     got = swap(send)

time: 157 us -> 158 us (level)
  Pallas kernels: 22.9 us -> 31.7 us
  waiting for transfers between devices: 33.6 us -> 26.6 us
  local copies, waits for them, and re-layouts: 10.1 us -> 3.95 us
  starting transfers between devices: 42.2 us -> 48.1 us
    pallas_call x9 -> x12, Pallas kernels: 22.9 us -> 31.7 us  [call(): pl.pallas_call(body, out_shape=[pltpu.VMEM(dims, kind) if keep else pltpu...]
    ppermute x3 -> x4, starting transfers between devices: 16.2 us -> 23.2 us  [swap(): return lax.ppermute(x, 'exp', swap_pairs)]
    ppermute x4, waiting for transfers between devices: 18.4 us -> 12.1 us  [trade_along(): return lax.ppermute(x, 'exp', pairs)]
    unnamed x47 -> x18, local copies, waits for them, and re-layouts: 10.1 us -> 3.95 us
    ppermute x3 -> x4, waiting for transfers between devices: 4.55 us -> 3.36 us  [swap(): return lax.ppermute(x, 'exp', swap_pairs)]
  transfers between devices with their start and end apart: 10 -> 11, of which waited for: 7 -> 7; matrix products, arithmetic and copies ran while one was open for 1% -> 1% of each run, Pallas kernels for 8% -> 11%
where the time goes in v2:
time: 158 us; the launch traced here: 157 us
  starting transfers between devices  48.1 us (30%)
  blocking collectives  45.3 us (29%)
  Pallas kernels  31.7 us (20%)
  waiting for transfers between devices  26.6 us (17%)
  local copies, waits for them, and re-layouts  3.95 us (2%)
    pallas_call x12, Pallas kernels, call(): pl.pallas_call(body, out_shape=[pltpu.VMEM(dims, kind) if keep else pltpu...  31.7 us
    ppermute x4, starting transfers between devices, swap(): return lax.ppermute(x, 'exp', swap_pairs)  23.2 us
    unnamed x1, blocking collectives  23.1 us
    all_to_all x1, blocking collectives, trade(): lax.all_to_all(x, 'ctx', split_axis=0, concat_axis=0, tiled=True)  22.3 us
    all_to_all x2, starting transfers between devices, trade(): lax.all_to_all(x, 'ctx', split_axis=0, concat_axis=0, tiled=True)  13.9 us
    ppermute x4, waiting for transfers between devices, trade_along(): return lax.ppermute(x, 'exp', pairs)  12.1 us
    ppermute x4, starting transfers between devices, trade_along(): return lax.ppermute(x, 'exp', pairs)  8.96 us
    all_to_all x2, waiting for transfers between devices, trade(): lax.all_to_all(x, 'ctx', split_axis=0, concat_axis=0, tiled=True)  7.91 us
  transfers between devices with their start and end apart: 11, of which 7 were waited for; matrix products, arithmetic and copies ran while one was open for 1% of the time, Pallas kernels for 11%

profile of v2, /device:TPU:33, one launch (start us, length us, event | category | flops | bytes accessed | tf_op | source)
XLA Modules:
  0.0 157.4 jit_solution(14552853232155310470)
XLA Ops:
  0.6 6.3 %shard_map.121.near = bf16[25,184,384]{2,1,0:T(8,128)(2,1)S(1)} custom-call(bf16[180,2,2880]{2,1,0:T(2,128)(2,1)} %bitcast.34, f32[180,2,90]{2,1,0:T(2,128)} %bitcast.41, bf16[180,2880]{1,0:T(8,128)(2,1)} %bitcast.35, f32[180,1,90]{2,1,0:T(1,128)} %bitcast.44, bf16[16,180]{1,0:T(8,128)(2,1)} %bitcast.45, bf16[16,180]{1,0:T(8,128)(2,1)} %bitcast.46), custom_call_target="tpu_custom_call" | custom-call | tf_op jit(solution)/shard_map/pallas_call | solution.py:50
  6.9 2.6 %collective-permute-start = (bf16[25,184,384]{2,1,0:T(8,128)(2,1)S(1)}, bf16[25,184,384]{2,1,0:T(8,128)(2,1)}, u32[]{:S(2)}, u32[]{:S(2)}) collective-permute-start(bf16[25,184,384]{2,1,0:T(8,128)(2,1)S(1)} %shard_map.121.near), channel_id=1, source_target_pairs={{0,1},{1,0},{2,3},{3,2},{4,5},{5,4},{6,7},{7,6},{8,9},{9,8},{10,11... | collective-permute-start | bytes 10598408 | tf_op jit(solution)/shard_map/ppermute | solution.py:268
  9.5 1.9 %collective-permute-start.1 = (bf16[180,256]{1,0:T(8,128)(2,1)}, bf16[180,256]{1,0:T(8,128)(2,1)}, u32[]{:S(2)}, u32[]{:S(2)}) collective-permute-start(bf16[180,256]{1,0:T(8,128)(2,1)} %bitcast.14.near), channel_id=1, source_target_pairs={{0,1},{1,0},{2,3},{3,2},{4,5},{5,4},{6,7},{7,6},{8,9},{9,8},{10,11... | collective-permute-start | bytes 276488 | tf_op jit(solution)/shard_map/ppermute | solution.py:268
  13.3 2.3 %collective-permute-done.1.far = bf16[180,256]{1,0:T(8,128)(2,1)} collective-permute-done((bf16[180,256]{1,0:T(8,128)(2,1)}, bf16[180,256]{1,0:T(8,128)(2,1)}, u32[]{:S(2)}, u32[]{:S(2)}) %collective-permute-start.1) | collective-permute-done | bytes 92192 | tf_op jit(solution)/shard_map/ppermute | solution.py:268
  15.6 2.3 %shard_map.123 = bf16[256,360]{1,0:T(8,128)(2,1)} custom-call(s32[3]{0:T(128)S(1)} %pad_add_fusion.where, bf16[256,256]{1,0:T(8,128)(2,1)} %get-tuple-element.18.one, bf16[180,256]{1,0:T(8,128)(2,1)} %bitcast.14.near, bf16[180,256]{1,0:T(8,128)(2,1)} %collective-permute-done.1.far), custom_call_target="tpu_custom_call" | custom-call | tf_op jit(solution)/shard_map/pallas_call | solution.py:50
  17.8 22.3 %all_to_all.15 = bf16[32,8,360]{2,1,0:T(8,128)(2,1)S(1)} all-to-all(bf16[32,8,360]{2,1,0:T(8,128)(2,1)} %bitcast.37), channel_id=1, replica_groups=mesh['ctx'=32,'exp'=16] {'ctx'}, dimensions={0} | all-to-all | bytes 368640 | tf_op jit(solution)/shard_map/all_to_all | solution.py:299
  40.1 2.1 %collective-permute-start.2 = (bf16[256,360]{1,0:T(8,128)(2,1)S(1)}, bf16[256,360]{1,0:T(8,128)(2,1)S(1)}, u32[]{:S(2)}, u32[]{:S(2)}) collective-permute-start(bf16[256,360]{1,0:T(8,128)(2,1)S(1)} %bitcast.39), channel_id=1, source_target_pairs={{0,2},{1,15},{2,0},{3,5},{4,6},{5,3},{6,4},{7,9},{8,10},{9,7},{10,... | collective-permute-start | bytes 552968 | tf_op jit(solution)/shard_map/ppermute | solution.py:276
  42.2 5.5 %collective-permute-done.2.second = bf16[256,360]{1,0:T(8,128)(2,1)S(1)} collective-permute-done((bf16[256,360]{1,0:T(8,128)(2,1)S(1)}, bf16[256,360]{1,0:T(8,128)(2,1)S(1)}, u32[]{:S(2)}, u32[]{:S(2)}) %collective-permute-start.2) | collective-permute-done | bytes 184352 | tf_op jit(solution)/shard_map/ppermute | solution.py:276
  48.7 1.9 %collective-permute-start.3 = (bf16[512,360]{1,0:T(8,128)(2,1)S(1)}, bf16[512,360]{1,0:T(8,128)(2,1)S(1)}, u32[]{:S(2)}, u32[]{:S(2)}) collective-permute-start(bf16[512,360]{1,0:T(8,128)(2,1)S(1)} %shard_map.124.first), channel_id=1, source_target_pairs={{0,14},{1,3},{2,4},{3,1},{4,2},{5,7},{6,8},{7,5},{8,6},{9,11},{10,... | collective-permute-start | bytes 1105928 | tf_op jit(solution)/shard_map/ppermute | solution.py:276
  51.4 5.8 %collective-permute-done.3.second = bf16[512,360]{1,0:T(8,128)(2,1)S(1)} collective-permute-done((bf16[512,360]{1,0:T(8,128)(2,1)S(1)}, bf16[512,360]{1,0:T(8,128)(2,1)S(1)}, u32[]{:S(2)}, u32[]{:S(2)}) %collective-permute-start.3) | collective-permute-done | bytes 368672 | tf_op jit(solution)/shard_map/ppermute | solution.py:276
  57.2 2.1 %collective-permute-start.4 = (bf16[512,360]{1,0:T(8,128)(2,1)S(1)}, bf16[512,360]{1,0:T(8,128)(2,1)}, u32[]{:S(2)}, u32[]{:S(2)}) collective-permute-start(bf16[512,360]{1,0:T(8,128)(2,1)S(1)} %collective-permute-done.3.second), channel_id=1, source_target_pairs={{0,2},{1,15},{2,0},{3,5},{4,6},{5,3},{6,4},{7,9},{8,10},{9,7},{10,... | collective-permute-start | bytes 1105928 | tf_op jit(solution)/shard_map/ppermute | solution.py:276
  59.3 7.0 %collective-permute-start.6 = (bf16[180,256]{1,0:T(8,128)(2,1)}, bf16[180,256]{1,0:T(8,128)(2,1)S(1)}, u32[]{:S(2)}, u32[]{:S(2)}) collective-permute-start(bf16[180,256]{1,0:T(8,128)(2,1)} %bitcast.42), channel_id=1, source_target_pairs={{0,1},{1,0},{2,3},{3,2},{4,5},{5,4},{6,7},{7,6},{8,9},{9,8},{10,11... | collective-permute-start | bytes 276488 | tf_op jit(solution)/shard_map/ppermute | solution.py:268
  67.0 2.9 %collective-permute-start.5 = (bf16[512,360]{1,0:T(8,128)(2,1)}, bf16[512,360]{1,0:T(8,128)(2,1)}, u32[]{:S(2)}, u32[]{:S(2)}) collective-permute-start(bf16[512,360]{1,0:T(8,128)(2,1)} %collective-permute-done.4.third), channel_id=1, source_target_pairs={{0,14},{1,3},{2,4},{3,1},{4,2},{5,7},{6,8},{7,5},{8,6},{9,11},{10,... | collective-permute-start | bytes 1105928 | tf_op jit(solution)/shard_map/ppermute | solution.py:276
  70.0 2.3 %shard_map.127 = bf16[256,360]{1,0:T(8,128)(2,1)} custom-call(s32[3]{0:T(128)S(1)} %pad_add_fusion.where, bf16[256,256]{1,0:T(8,128)(2,1)} %get-tuple-element.18.one, bf16[256,256]{1,0:T(8,128)(2,1)} %get-tuple-element.19.pick, bf16[256,256]{1,0:T(8,128)(2,1)} %get-tuple-element.20.weigh, bf16[180,256]{1,0:T(8,128)(2,1)} %bitcast.43, ...), custom_call_target="tpu_custom_call" | custom-call | tf_op jit(solution)/shard_map/pallas_call | solution.py:50
  72.3 4.9 %all-to-all-start.1 = ((bf16[32,8,360]{2,1,0:T(8,128)(2,1)}), bf16[32,8,360]{2,1,0:T(8,128)(2,1)}, u32[]{:S(2)}, u32[]{:S(2)}) async-start(bf16[32,8,360]{2,1,0:T(8,128)(2,1)} %bitcast.38), calls=%async_computation.1 | async-start | bytes 393216 | tf_op jit(solution)/shard_map/all_to_all | solution.py:299
  78.2 4.3 %shard_map.125.before = f32[2,2,256,180]{3,2,1,0:T(8,128)} custom-call(s32[3]{0:T(128)S(1)} %pad_add_fusion.where, bf16[25,184,384]{2,1,0:T(8,128)(2,1)S(1)} %shard_map.121.near, bf16[25,184,384]{2,1,0:T(8,128)(2,1)} %collective-permute-done.far, bf16[512,360]{1,0:T(8,128)(2,1)S(1)} %copy-done.1, bf16[512,360]{1,0:T(8,128)(2,1)} %copy-done.6), custom_call_target="tpu_custom_call" | custom-call | tf_op jit(solution)/shard_map/pallas_call | solution.py:50
  82.5 4.2 %shard_map.126.sums = f32[2,2,256,180]{3,2,1,0:T(8,128)} custom-call(s32[3]{0:T(128)S(1)} %pad_add_fusion.where, bf16[25,184,384]{2,1,0:T(8,128)(2,1)S(1)} %shard_map.121.near, bf16[25,184,384]{2,1,0:T(8,128)(2,1)} %collective-permute-done.far, bf16[512,360]{1,0:T(8,128)(2,1)} %collective-permute-done.4.third, f32[2,2,256,180]{3,2,1,0:T(8,128)} %shard_map.125.before), custom_call_target="tpu_custom_call" | custom-call | tf_op jit(solution)/shard_map/pallas_call | solution.py:50
  86.7 5.6 %shard_map.128 = (bf16[256,180]{1,0:T(8,128)(2,1)}, bf16[256,180]{1,0:T(8,128)(2,1)}, bf16[16,360]{1,0:T(8,128)(2,1)}, bf16[2208,384]{1,0:T(8,128)(2,1)}) custom-call(s32[3]{0:T(128)S(1)} %pad_add_fusion.where, bf16[25,184,384]{2,1,0:T(8,128)(2,1)S(1)} %shard_map.121.near, bf16[25,184,384]{2,1,0:T(8,128)(2,1)} %collective-permute-done.far, ...), custom_call_target="tpu_custom_call" | custom-call | tf_op jit(solution)/shard_map/pallas_call | solution.py:50
  92.3 23.1 %fusion = bf16[288,384]{1,0:T(8,128)(2,1)S(1)} fusion(bf16[2208,384]{1,0:T(8,128)(2,1)} %get-tuple-element.21), kind=kCustom, calls=%all-reduce-scatter | all-reduce-scatter fusion | flops 884737 | bytes 1918976
  115.4 2.1 %collective-permute-start.8 = (bf16[84,384]{1,0:T(8,128)(2,1)S(1)}, bf16[84,384]{1,0:T(8,128)(2,1)S(1)}, u32[]{:S(2)}, u32[]{:S(2)}) collective-permute-start(bf16[84,384]{1,0:T(8,128)(2,1)S(1)} %slice), channel_id=1, source_target_pairs={{0,2},{2,4},{4,6},{6,8},{8,10},{10,12},{12,14},{1,3},{3,5},{5,7},{... | collective-permute-start | bytes 193544
  119.4 3.2 %collective-permute-done.8 = bf16[84,384]{1,0:T(8,128)(2,1)S(1)} collective-permute-done((bf16[84,384]{1,0:T(8,128)(2,1)S(1)}, bf16[84,384]{1,0:T(8,128)(2,1)S(1)}, u32[]{:S(2)}, u32[]{:S(2)}) %collective-permute-start.8) | collective-permute-done | bytes 64544
  124.6 9.0 %all-to-all-start.2 = ((bf16[32,8,360]{2,1,0:T(8,128)(2,1)}), bf16[32,8,360]{2,1,0:T(8,128)(2,1)S(1)}, u32[]{:S(2)}, u32[]{:S(2)}) async-start(bf16[32,8,360]{2,1,0:T(8,128)(2,1)} %bitcast.36), calls=%async_computation.2 | async-start | bytes 393216 | tf_op jit(solution)/shard_map/all_to_all | solution.py:299
  135.1 7.9 %all-to-all-done.2 = bf16[32,8,360]{2,1,0:T(8,128)(2,1)S(1)} async-done(((bf16[32,8,360]{2,1,0:T(8,128)(2,1)}), bf16[32,8,360]{2,1,0:T(8,128)(2,1)S(1)}, u32[]{:S(2)}, u32[]{:S(2)}) %all-to-all-start.2) | async-done | bytes 184352 | tf_op jit(solution)/shard_map/all_to_all | solution.py:299
  143.9 11.7 %collective-permute-start.7 = (f32[216,256]{1,0:T(8,128)S(1)}, f32[216,256]{1,0:T(8,128)S(1)}, u32[]{:S(2)}, u32[]{:S(2)}) collective-permute-start(f32[216,256]{1,0:T(8,128)S(1)} %get-tuple-element.29), channel_id=1, source_target_pairs={{0,1},{1,0},{2,3},{3,2},{4,5},{5,4},{6,7},{7,6},{8,9},{9,8},{10,11... | collective-permute-start | bytes 663560 | tf_op jit(solution)/shard_map/ppermute | solution.py:268
  (31 shorter events, 12.6 us)
Async XLA Ops:
  6.9 70.3 %collective-permute-start = (bf16[25,184,384]{2,1,0:T(8,128)(2,1)S(1)}, bf16[25,184,384]{2,1,0:T(8,128)(2,1)}, u32[]{:S(2)}, u32[]{:S(2)}) collective-permute-start(bf16[25,184,384]{2,1,0:T(8,128)(2,1)S(1)} %shard_map.121.near), channel_id=1, source_target_pairs={{0,1},{1,0},{2,3},{3,2},{4,5},{5,4},{6,7},{7,6},{8,9},{9,8},{10,11... | collective-permute-start | bytes 10598408 | tf_op jit(solution)/shard_map/ppermute | solution.py:268
  9.5 6.1 %collective-permute-start.1 = (bf16[180,256]{1,0:T(8,128)(2,1)}, bf16[180,256]{1,0:T(8,128)(2,1)}, u32[]{:S(2)}, u32[]{:S(2)}) collective-permute-start(bf16[180,256]{1,0:T(8,128)(2,1)} %bitcast.14.near), channel_id=1, source_target_pairs={{0,1},{1,0},{2,3},{3,2},{4,5},{5,4},{6,7},{7,6},{8,9},{9,8},{10,11... | collective-permute-start | bytes 276488 | tf_op jit(solution)/shard_map/ppermute | solution.py:268
  40.1 7.6 %copy-start.5 = (bf16[32,8,360]{2,1,0:T(8,128)(2,1)}, bf16[32,8,360]{2,1,0:T(8,128)(2,1)S(1)}, u32[]{:S(2)}) copy-start(bf16[32,8,360]{2,1,0:T(8,128)(2,1)S(1)} %all_to_all.15) | copy-start | bytes 552964
  40.1 7.6 %collective-permute-start.2 = (bf16[256,360]{1,0:T(8,128)(2,1)S(1)}, bf16[256,360]{1,0:T(8,128)(2,1)S(1)}, u32[]{:S(2)}, u32[]{:S(2)}) collective-permute-start(bf16[256,360]{1,0:T(8,128)(2,1)S(1)} %bitcast.39), channel_id=1, source_target_pairs={{0,2},{1,15},{2,0},{3,5},{4,6},{5,3},{6,4},{7,9},{8,10},{9,7},{10,... | collective-permute-start | bytes 552968 | tf_op jit(solution)/shard_map/ppermute | solution.py:276
  48.7 8.5 %collective-permute-start.3 = (bf16[512,360]{1,0:T(8,128)(2,1)S(1)}, bf16[512,360]{1,0:T(8,128)(2,1)S(1)}, u32[]{:S(2)}, u32[]{:S(2)}) collective-permute-start(bf16[512,360]{1,0:T(8,128)(2,1)S(1)} %shard_map.124.first), channel_id=1, source_target_pairs={{0,14},{1,3},{2,4},{3,1},{4,2},{5,7},{6,8},{7,5},{8,6},{9,11},{10,... | collective-permute-start | bytes 1105928 | tf_op jit(solution)/shard_map/ppermute | solution.py:276
  50.6 0.8 copy-start
  57.2 12.7 %copy-start.6 = (bf16[512,360]{1,0:T(8,128)(2,1)}, bf16[512,360]{1,0:T(8,128)(2,1)S(1)}, u32[]{:S(2)}) copy-start(bf16[512,360]{1,0:T(8,128)(2,1)S(1)} %collective-permute-done.3.second) | copy-start | bytes 1105924
  57.2 9.8 %collective-permute-start.4 = (bf16[512,360]{1,0:T(8,128)(2,1)S(1)}, bf16[512,360]{1,0:T(8,128)(2,1)}, u32[]{:S(2)}, u32[]{:S(2)}) collective-permute-start(bf16[512,360]{1,0:T(8,128)(2,1)S(1)} %collective-permute-done.3.second), channel_id=1, source_target_pairs={{0,2},{1,15},{2,0},{3,5},{4,6},{5,3},{6,4},{7,9},{8,10},{9,7},{10,... | collective-permute-start | bytes 1105928 | tf_op jit(solution)/shard_map/ppermute | solution.py:276
  59.3 10.6 %collective-permute-start.6 = (bf16[180,256]{1,0:T(8,128)(2,1)}, bf16[180,256]{1,0:T(8,128)(2,1)S(1)}, u32[]{:S(2)}, u32[]{:S(2)}) collective-permute-start(bf16[180,256]{1,0:T(8,128)(2,1)} %bitcast.42), channel_id=1, source_target_pairs={{0,1},{1,0},{2,3},{3,2},{4,5},{5,4},{6,7},{7,6},{8,9},{9,8},{10,11... | collective-permute-start | bytes 276488 | tf_op jit(solution)/shard_map/ppermute | solution.py:268
  67.0 19.6 %collective-permute-start.5 = (bf16[512,360]{1,0:T(8,128)(2,1)}, bf16[512,360]{1,0:T(8,128)(2,1)}, u32[]{:S(2)}, u32[]{:S(2)}) collective-permute-start(bf16[512,360]{1,0:T(8,128)(2,1)} %collective-permute-done.4.third), channel_id=1, source_target_pairs={{0,14},{1,3},{2,4},{3,1},{4,2},{5,7},{6,8},{7,5},{8,6},{9,11},{10,... | collective-permute-start | bytes 1105928 | tf_op jit(solution)/shard_map/ppermute | solution.py:276
  72.3 14.4 %all-to-all-start.1 = ((bf16[32,8,360]{2,1,0:T(8,128)(2,1)}), bf16[32,8,360]{2,1,0:T(8,128)(2,1)}, u32[]{:S(2)}, u32[]{:S(2)}) async-start(bf16[32,8,360]{2,1,0:T(8,128)(2,1)} %bitcast.38), calls=%async_computation.1 | async-start | bytes 393216 | tf_op jit(solution)/shard_map/all_to_all | solution.py:299
  77.2 1.0 copy-start.1
  92.3 31.2 %copy-start.4 = (bf16[16,360]{1,0:T(8,128)(2,1)S(1)}, bf16[16,360]{1,0:T(8,128)(2,1)}, u32[]{:S(2)}) copy-start(bf16[16,360]{1,0:T(8,128)(2,1)} %get-tuple-element.22.up) | copy-start | bytes 34564
  115.4 27.7 %copy-start.2 = (bf16[256,256]{1,0:T(8,128)(2,1)S(1)}, bf16[256,256]{1,0:T(8,128)(2,1)}, u32[]{:S(2)}) copy-start(bf16[256,256]{1,0:T(8,128)(2,1)} %get-tuple-element.19.pick) | copy-start | bytes 393220
  115.4 27.7 %copy-start.3 = (bf16[256,256]{1,0:T(8,128)(2,1)S(1)}, bf16[256,256]{1,0:T(8,128)(2,1)}, u32[]{:S(2)}) copy-start(bf16[256,256]{1,0:T(8,128)(2,1)} %get-tuple-element.20.weigh) | copy-start | bytes 393220
  115.4 7.2 %collective-permute-start.8 = (bf16[84,384]{1,0:T(8,128)(2,1)S(1)}, bf16[84,384]{1,0:T(8,128)(2,1)S(1)}, u32[]{:S(2)}, u32[]{:S(2)}) collective-permute-start(bf16[84,384]{1,0:T(8,128)(2,1)S(1)} %slice), channel_id=1, source_target_pairs={{0,2},{2,4},{4,6},{6,8},{8,10},{10,12},{12,14},{1,3},{3,5},{5,7},{... | collective-permute-start | bytes 193544
  124.6 18.4 %all-to-all-start.2 = ((bf16[32,8,360]{2,1,0:T(8,128)(2,1)}), bf16[32,8,360]{2,1,0:T(8,128)(2,1)S(1)}, u32[]{:S(2)}, u32[]{:S(2)}) async-start(bf16[32,8,360]{2,1,0:T(8,128)(2,1)} %bitcast.36), calls=%async_computation.2 | async-start | bytes 393216 | tf_op jit(solution)/shard_map/all_to_all | solution.py:299
  143.9 12.8 %collective-permute-start.7 = (f32[216,256]{1,0:T(8,128)S(1)}, f32[216,256]{1,0:T(8,128)S(1)}, u32[]{:S(2)}, u32[]{:S(2)}) collective-permute-start(f32[216,256]{1,0:T(8,128)S(1)} %get-tuple-element.29), channel_id=1, source_target_pairs={{0,1},{1,0},{2,3},{3,2},{4,5},{5,4},{6,7},{7,6},{8,9},{9,8},{10,11... | collective-permute-start | bytes 663560 | tf_op jit(solution)/shard_map/ppermute | solution.py:268

commit v3 on v2

--- a/solution.py
+++ b/solution.py
@@ -38,7 +38,7 @@
     return -(-n // 128) * 128
 
 
-def call(body, out_shape, *args, scalars=1, keep=False, local=(), free=(), scratch=()):
+def call(body, out_shape, *args, scalars=1, keep=(), local=(), free=(), scratch=()):
     smem = pl.BlockSpec(memory_space=pltpu.SMEM)
     vmem = pl.BlockSpec(memory_space=pltpu.VMEM)
     args = [
@@ -50,7 +50,8 @@
     return pl.pallas_call(
         body,
         out_shape=[
-            pltpu.VMEM(dims, kind) if keep else pltpu.HBM(dims, kind) for dims, kind in out_shape
+            (pltpu.VMEM if keep is True or i in keep else pltpu.HBM)(dims, kind)
+            for i, (dims, kind) in enumerate(out_shape)
         ],
         in_specs=[smem if i < scalars else vmem for i in range(len(args))],
         out_specs=[vmem for _ in out_shape],
@@ -59,7 +60,7 @@
     )(*args)
 
 
-def assign(where, ids, weights, pick, weigh, one):
+def assign(where, ids, weights, pick, weigh, one, again):
     side = where[1]
     slots, count = pick.shape
     flight = slots // HALF
@@ -73,29 +74,34 @@
     before = dot(named.astype(BF), earlier, NN) - (side * HALF).astype(F32)
     slot = iota((flight, HALF, count), 1).astype(F32)
     taken = (before[:, None, :] == slot) & (named[:, None, :] > 0.5)
-    one[...] = jnp.where(taken, 1.0, 0.0).reshape(slots, count).astype(BF)
+    chosen = jnp.where(taken, 1.0, 0.0).reshape(slots, count).astype(BF)
+    one[...] = chosen
+    again[...] = chosen
     scaled = jnp.where(taken, weight[:, None, :], 0.0).reshape(slots, count)
     upper = scaled.astype(BF)
     pick[...] = upper
     weigh[...] = (scaled - upper.astype(F32)).astype(BF)
 
 
-def features(where, near, far):
+def features(where, near, far, second):
     side = where[1]
-    width = near.shape[0]
-    row, col = iota((2 * width, width), 0), iota((2 * width, width), 1)
-    left = jnp.where(row == col + side * width, 1.0, 0.0).astype(BF)
-    right = jnp.where(row == col + (1 - side) * width, 1.0, 0.0).astype(BF)
+    both = near.shape[0]
+    width = both // 2
+    row, col = iota((both, both), 0), iota((both, both), 1)
+    inside = (col >= width) if second else (col < width)
+    at = row + width if second else row
+    left = jnp.where((at == col + side * width) & inside, 1.0, 0.0).astype(BF)
+    right = jnp.where((at == col + (1 - side) * width) & inside, 1.0, 0.0).astype(BF)
     return (dot(left, near[...], NN) + dot(right, far[...], NN)).astype(BF)
 
 
 def select_rows(where, one, near, far, rows):
-    rows[...] = dot(one[...], features(where, near, far), NT).astype(BF)
+    rows[...] = dot(one[...], features(where, near, far, False), NT).astype(BF)
 
 
 def select_grads(where, one, pick, weigh, near, far, grads):
     factor = jnp.sum(pick[...].astype(F32) + weigh[...].astype(F32), axis=1, keepdims=True)
-    grads[...] = (factor * dot(one[...], features(where, near, far), NT)).astype(BF)
+    grads[...] = (factor * dot(one[...], features(where, near, far, True), NT)).astype(BF)
 
 
 def join(first, second, out):
@@ -189,12 +195,18 @@
     both = dot(near[3 * parts, :rank, :half], here, NN) + dot(far[3 * parts, :rank, :half], there, NN)
     both = both.astype(BF)
     up[...] = both
-    back = dot(both, grads[...], NT)
+    few = rank // 2
+    free = pad - few
+    spread = jnp.where(
+        iota((pad, rank), 0) - free == iota((pad, rank), 1) - few, 1.0, 0.0
+    ) * jnp.where(iota((pad, rank), 0) >= free, 1.0, 0.0)
+    beside = dot(grads[...], dot(spread.astype(BF), both, NN).astype(BF), NT)
+    back = dot(both, grads[...], NT)[:few]
     for a in range(parts):
         total = dot(acts[0], near[2 * parts + a, :hidden, :], NN) + dot(acts[1], far[2 * parts + a, :hidden, :], NN)
-        wide[a * tall : a * tall + count, :] = total
+        wide[a * tall : a * tall + count, :] = total + beside
         wide[a * tall + count : (a + 1) * tall, :] = jnp.zeros((tall - count, pad), F32)
-        wide[a * tall + count : a * tall + count + rank, :count] = back
+        wide[a * tall + count : a * tall + count + few, :count] = back
     out[...] = wide[...].astype(BF)
 
 
@@ -212,14 +224,17 @@
     side = where[1]
     count, piece = grads.shape
     rank, half = left.shape
-    back = (ADAPTER_SCALE * total[count : count + rank, :count].astype(F32)).astype(BF)
-    left[...] = dot(back, act_near[...], NN)
+    few = rank // 2
+    free = total.shape[1] - few
+    back = total[count : count + few, :count]
+    send[...] = jnp.zeros(send.shape, F32)
+    for act, at in ((act_near, left), (act_far, send)):
+        at[:few, :half] = ADAPTER_SCALE * dot(back, act[...], NN)
+        at[few:rank, :half] = ADAPTER_SCALE * dot(total[:count, :], act[...], TN)[free:]
     product = dot(total[:count, :], grads[...], TN)
     whole = ADAPTER_SCALE * product[piece : piece + rank]
     first, second = whole[:, :half], whole[:, half:]
     right[...] = jnp.where(side == 0, first, second)
-    send[...] = jnp.zeros(send.shape, F32)
-    send[:rank, :half] = dot(back, act_far[...], NN)
     send[rank:, :half] = jnp.where(side == 0, second, first)
 
 
@@ -275,23 +290,24 @@
                 pairs.append((2 * y + c, 2 * ((y + way) % ring) + c))
         return lax.ppermute(x, "exp", pairs)
 
-    width, count = tokens.shape[1], tokens.shape[0]
+    count, width = tokens.shape
     slots = flight * HALF
     hidden, _ = down_weight_blocks.shape[1:]
     piece = 2 * width
     rank = adapter_up_matrix.shape[1]
     pad = up128(piece + rank)
 
-    tok, cot = tokens.T, cotangent.T
-    tok_far = swap(tok)
-    cot_far = swap(cot)
-    pick, weigh, one = call(
-        assign, [((slots, count), BF)] * 3, where, expert_indices.T, routing_weights.T,
-    )
-    (rows,) = call(select_rows, [((slots, piece), BF)], where, one, tok, tok_far, local=(3,))
+    own = jnp.concatenate([tokens.T, cotangent.T], axis=0)
+    other = swap(own)
+    pick, weigh, one, again = call(
+        assign, [((slots, count), BF)] * 4, where, expert_indices.T, routing_weights.T,
+        keep=(2,),
+    )
+    (rows,) = call(
+        select_rows, [((slots, piece), BF)], where, one, own, other, local=(1, 2, 3)
+    )
     (grads,) = call(
-        select_grads, [((slots, piece), BF)], where, one, pick, weigh, cot, cot_far,
-        local=(5,),
+        select_grads, [((slots, piece), BF)], where, again, pick, weigh, own, other
     )
 
     def trade(x):
@@ -325,7 +341,7 @@
     (sums,) = call(
         project_more, [((2, 2, slots, hidden), F32)], where, near, far, third, sums, local=(1, 2)
     )
-    tall = slots + rank + 4
+    tall = slots + rank // 2 + 4
     act_near, act_far, up, partial = call(
         expert,
         [((slots, hidden), BF)] * 2 + [((rank, piece), BF), ((ring * tall, pad), BF)],

time: 158 us -> 158 us (level)
  starting transfers between devices: 48.1 us -> 41.1 us
  waiting for transfers between devices: 26.6 us -> 32.2 us
    ppermute x4, waiting for transfers between devices: 12.1 us -> 19.1 us  [trade_along(): return lax.ppermute(x, 'exp', pairs)]
    ppermute x4 -> x3, starting transfers between devices: 23.2 us -> 16.8 us  [swap(): return lax.ppermute(x, 'exp', swap_pairs)]
    unnamed x18 -> x22, local copies, waits for them, and re-layouts: 3.95 us -> 4.66 us
    ppermute x4 -> x3, waiting for transfers between devices: 3.36 us -> 2.76 us  [swap(): return lax.ppermute(x, 'exp', swap_pairs)]
  transfers between devices with their start and end apart: 11 -> 10, of which waited for: 7 -> 7; matrix products, arithmetic and copies ran while one was open for 1% -> 1% of each run, Pallas kernels for 11% -> 11%
where the time goes in v3:
time: 158 us
  blocking collectives  44.8 us (28%)
  starting transfers between devices  41.1 us (26%)
  Pallas kernels  32.6 us (21%)
  waiting for transfers between devices  32.2 us (20%)
  local copies, waits for them, and re-layouts  4.66 us (3%)
    pallas_call x12, Pallas kernels, call(): pl.pallas_call(body, out_shape=[(pltpu.VMEM if keep is True or i in keep...  32.6 us
    unnamed x1, blocking collectives  22.5 us
    all_to_all x1, blocking collectives, trade(): lax.all_to_all(x, 'ctx', split_axis=0, concat_axis=0, tiled=True)  22.3 us
    ppermute x4, waiting for transfers between devices, trade_along(): return lax.ppermute(x, 'exp', pairs)  19.1 us
    ppermute x3, starting transfers between devices, swap(): return lax.ppermute(x, 'exp', swap_pairs)  16.8 us
    all_to_all x2, starting transfers between devices, trade(): lax.all_to_all(x, 'ctx', split_axis=0, concat_axis=0, tiled=True)  14.3 us
    ppermute x4, starting transfers between devices, trade_along(): return lax.ppermute(x, 'exp', pairs)  7.96 us
    all_to_all x2, waiting for transfers between devices, trade(): lax.all_to_all(x, 'ctx', split_axis=0, concat_axis=0, tiled=True)  7.79 us
  transfers between devices with their start and end apart: 10, of which 7 were waited for; matrix products, arithmetic and copies ran while one was open for 1% of the time, Pallas kernels for 11%

profile of v3, /device:TPU:33, one launch (start us, length us, event | category | flops | bytes accessed | tf_op | source)
XLA Modules:
  0.0 157.7 jit_solution(581280164094068280)
XLA Ops:
  0.7 6.3 %shard_map.121.near = bf16[25,184,384]{2,1,0:T(8,128)(2,1)S(1)} custom-call(bf16[180,2,2880]{2,1,0:T(2,128)(2,1)} %bitcast.34, f32[180,2,90]{2,1,0:T(2,128)} %bitcast.41, bf16[180,2880]{1,0:T(8,128)(2,1)} %bitcast.35, f32[180,1,90]{2,1,0:T(1,128)} %bitcast.44, bf16[16,180]{1,0:T(8,128)(2,1)} %bitcast.45, bf16[16,180]{1,0:T(8,128)(2,1)} %bitcast.46), custom_call_target="tpu_custom_call" | custom-call | tf_op jit(solution)/shard_map/pallas_call | solution.py:50
  6.9 2.6 %collective-permute-start = (bf16[25,184,384]{2,1,0:T(8,128)(2,1)S(1)}, bf16[25,184,384]{2,1,0:T(8,128)(2,1)}, u32[]{:S(2)}, u32[]{:S(2)}) collective-permute-start(bf16[25,184,384]{2,1,0:T(8,128)(2,1)S(1)} %shard_map.121.near), channel_id=1, source_target_pairs={{0,1},{1,0},{2,3},{3,2},{4,5},{5,4},{6,7},{7,6},{8,9},{9,8},{10,11... | collective-permute-start | bytes 10598408 | tf_op jit(solution)/shard_map/ppermute | solution.py:283
  10.3 1.9 %collective-permute-start.1 = (bf16[360,256]{1,0:T(8,128)(2,1)}, bf16[360,256]{1,0:T(8,128)(2,1)}, u32[]{:S(2)}, u32[]{:S(2)}) collective-permute-start(bf16[360,256]{1,0:T(8,128)(2,1)} %pad_maximum_fusion.near), channel_id=1, source_target_pairs={{0,1},{1,0},{2,3},{3,2},{4,5},{5,4},{6,7},{7,6},{8,9},{9,8},{10,11... | collective-permute-start | bytes 552968 | tf_op jit(solution)/shard_map/ppermute | solution.py:283
  12.3 1.8 %shard_map.122 = (bf16[256,256]{1,0:T(8,128)(2,1)}, bf16[256,256]{1,0:T(8,128)(2,1)}, bf16[256,256]{1,0:T(8,128)(2,1)S(1)}, bf16[256,256]{1,0:T(8,128)(2,1)}) custom-call(s32[3]{0:T(128)S(1)} %pad_add_fusion.where, s32[4,256]{1,0:T(4,128)} %bitcast.47, f32[4,256]{1,0:T(4,128)} %bitcast.48), custom_call_target="tpu_custom_call" | custom-call | tf_op jit(solution)/shard_map/pallas_call | solution.py:50
  15.7 2.3 %shard_map.123 = bf16[256,360]{1,0:T(8,128)(2,1)} custom-call(s32[3]{0:T(128)S(1)} %pad_add_fusion.where, bf16[256,256]{1,0:T(8,128)(2,1)S(1)} %get-tuple-element.19.one, bf16[360,256]{1,0:T(8,128)(2,1)} %pad_maximum_fusion.near, bf16[360,256]{1,0:T(8,128)(2,1)} %collective-permute-done.1.far), custom_call_target="tpu_custom_call" | custom-call | tf_op jit(solution)/shard_map/pallas_call | solution.py:50
  18.1 22.3 %all_to_all.15 = bf16[32,8,360]{2,1,0:T(8,128)(2,1)S(1)} all-to-all(bf16[32,8,360]{2,1,0:T(8,128)(2,1)} %bitcast.40), channel_id=1, replica_groups=mesh['ctx'=32,'exp'=16] {'ctx'}, dimensions={0} | all-to-all | bytes 368640 | tf_op jit(solution)/shard_map/all_to_all | solution.py:315
  40.4 2.1 %collective-permute-start.2 = (bf16[256,360]{1,0:T(8,128)(2,1)S(1)}, bf16[256,360]{1,0:T(8,128)(2,1)S(1)}, u32[]{:S(2)}, u32[]{:S(2)}) collective-permute-start(bf16[256,360]{1,0:T(8,128)(2,1)S(1)} %bitcast.38), channel_id=1, source_target_pairs={{0,2},{1,15},{2,0},{3,5},{4,6},{5,3},{6,4},{7,9},{8,10},{9,7},{10,... | collective-permute-start | bytes 552968 | tf_op jit(solution)/shard_map/ppermute | solution.py:291
  42.4 5.5 %collective-permute-done.2.second = bf16[256,360]{1,0:T(8,128)(2,1)S(1)} collective-permute-done((bf16[256,360]{1,0:T(8,128)(2,1)S(1)}, bf16[256,360]{1,0:T(8,128)(2,1)S(1)}, u32[]{:S(2)}, u32[]{:S(2)}) %collective-permute-start.2) | collective-permute-done | bytes 184352 | tf_op jit(solution)/shard_map/ppermute | solution.py:291
  48.9 1.9 %collective-permute-start.3 = (bf16[512,360]{1,0:T(8,128)(2,1)S(1)}, bf16[512,360]{1,0:T(8,128)(2,1)S(1)}, u32[]{:S(2)}, u32[]{:S(2)}) collective-permute-start(bf16[512,360]{1,0:T(8,128)(2,1)S(1)} %shard_map.124.first), channel_id=1, source_target_pairs={{0,14},{1,3},{2,4},{3,1},{4,2},{5,7},{6,8},{7,5},{8,6},{9,11},{10,... | collective-permute-start | bytes 1105928 | tf_op jit(solution)/shard_map/ppermute | solution.py:291
  51.6 5.8 %collective-permute-done.3.second = bf16[512,360]{1,0:T(8,128)(2,1)S(1)} collective-permute-done((bf16[512,360]{1,0:T(8,128)(2,1)S(1)}, bf16[512,360]{1,0:T(8,128)(2,1)S(1)}, u32[]{:S(2)}, u32[]{:S(2)}) %collective-permute-start.3) | collective-permute-done | bytes 368672 | tf_op jit(solution)/shard_map/ppermute | solution.py:291
  58.2 2.1 %collective-permute-start.4 = (bf16[512,360]{1,0:T(8,128)(2,1)S(1)}, bf16[512,360]{1,0:T(8,128)(2,1)}, u32[]{:S(2)}, u32[]{:S(2)}) collective-permute-start(bf16[512,360]{1,0:T(8,128)(2,1)S(1)} %collective-permute-done.3.second), channel_id=1, source_target_pairs={{0,2},{1,15},{2,0},{3,5},{4,6},{5,3},{6,4},{7,9},{8,10},{9,7},{10,... | collective-permute-start | bytes 1105928 | tf_op jit(solution)/shard_map/ppermute | solution.py:291
  60.3 7.8 %collective-permute-done.4.third = bf16[512,360]{1,0:T(8,128)(2,1)} collective-permute-done((bf16[512,360]{1,0:T(8,128)(2,1)S(1)}, bf16[512,360]{1,0:T(8,128)(2,1)}, u32[]{:S(2)}, u32[]{:S(2)}) %collective-permute-start.4) | collective-permute-done | bytes 368672 | tf_op jit(solution)/shard_map/ppermute | solution.py:291
  68.1 1.9 %collective-permute-start.5 = (bf16[512,360]{1,0:T(8,128)(2,1)}, bf16[512,360]{1,0:T(8,128)(2,1)}, u32[]{:S(2)}, u32[]{:S(2)}) collective-permute-start(bf16[512,360]{1,0:T(8,128)(2,1)} %collective-permute-done.4.third), channel_id=1, source_target_pairs={{0,14},{1,3},{2,4},{3,1},{4,2},{5,7},{6,8},{7,5},{8,6},{9,11},{10,... | collective-permute-start | bytes 1105928 | tf_op jit(solution)/shard_map/ppermute | solution.py:291
  70.0 2.6 %shard_map.127 = bf16[256,360]{1,0:T(8,128)(2,1)} custom-call(s32[3]{0:T(128)S(1)} %pad_add_fusion.where, bf16[256,256]{1,0:T(8,128)(2,1)} %get-tuple-element.20.one, bf16[256,256]{1,0:T(8,128)(2,1)} %get-tuple-element.21.pick, bf16[256,256]{1,0:T(8,128)(2,1)} %get-tuple-element.22.weigh, bf16[360,256]{1,0:T(8,128)(2,1)} %pad_maximum_fusion.near, ...), custom_call_target="tpu_custom_call" | custom-call | tf_op jit(solution)/shard_map/pallas_call | solution.py:50
  72.5 5.9 %all-to-all-start.1 = ((bf16[32,8,360]{2,1,0:T(8,128)(2,1)}), bf16[32,8,360]{2,1,0:T(8,128)(2,1)}, u32[]{:S(2)}, u32[]{:S(2)}) async-start(bf16[32,8,360]{2,1,0:T(8,128)(2,1)} %bitcast.36), calls=%async_computation.1 | async-start | bytes 393216 | tf_op jit(solution)/shard_map/all_to_all | solution.py:315
  79.4 4.3 %shard_map.125.before = f32[2,2,256,180]{3,2,1,0:T(8,128)} custom-call(s32[3]{0:T(128)S(1)} %pad_add_fusion.where, bf16[25,184,384]{2,1,0:T(8,128)(2,1)S(1)} %shard_map.121.near, bf16[25,184,384]{2,1,0:T(8,128)(2,1)} %collective-permute-done.far, bf16[512,360]{1,0:T(8,128)(2,1)S(1)} %copy-done.1, bf16[512,360]{1,0:T(8,128)(2,1)} %copy-done.6), custom_call_target="tpu_custom_call" | custom-call | tf_op jit(solution)/shard_map/pallas_call | solution.py:50
  83.7 4.2 %shard_map.126.sums = f32[2,2,256,180]{3,2,1,0:T(8,128)} custom-call(s32[3]{0:T(128)S(1)} %pad_add_fusion.where, bf16[25,184,384]{2,1,0:T(8,128)(2,1)S(1)} %shard_map.121.near, bf16[25,184,384]{2,1,0:T(8,128)(2,1)} %collective-permute-done.far, bf16[512,360]{1,0:T(8,128)(2,1)} %collective-permute-done.4.third, f32[2,2,256,180]{3,2,1,0:T(8,128)} %shard_map.125.before), custom_call_target="tpu_custom_call" | custom-call | tf_op jit(solution)/shard_map/pallas_call | solution.py:50
  87.9 6.0 %shard_map.128 = (bf16[256,180]{1,0:T(8,128)(2,1)}, bf16[256,180]{1,0:T(8,128)(2,1)}, bf16[16,360]{1,0:T(8,128)(2,1)}, bf16[2144,384]{1,0:T(8,128)(2,1)}) custom-call(s32[3]{0:T(128)S(1)} %pad_add_fusion.where, bf16[25,184,384]{2,1,0:T(8,128)(2,1)S(1)} %shard_map.121.near, bf16[25,184,384]{2,1,0:T(8,128)(2,1)} %collective-permute-done.far, ...), custom_call_target="tpu_custom_call" | custom-call | tf_op jit(solution)/shard_map/pallas_call | solution.py:50
  93.9 22.5 %fusion = bf16[272,384]{1,0:T(8,128)(2,1)S(1)} fusion(bf16[2144,384]{1,0:T(8,128)(2,1)} %get-tuple-element.23), kind=kCustom, calls=%all-reduce-scatter | all-reduce-scatter fusion | flops 835585 | bytes 1857536
  116.5 2.1 %collective-permute-start.7 = (bf16[28,384]{1,0:T(8,128)(2,1)S(1)}, bf16[28,384]{1,0:T(8,128)(2,1)S(1)}, u32[]{:S(2)}, u32[]{:S(2)}) collective-permute-start(bf16[28,384]{1,0:T(8,128)(2,1)S(1)} %slice), channel_id=1, source_target_pairs={{0,2},{2,4},{4,6},{6,8},{8,10},{10,12},{12,14},{1,3},{3,5},{5,7},{... | collective-permute-start | bytes 64520
  120.5 2.5 %collective-permute-done.7 = bf16[28,384]{1,0:T(8,128)(2,1)S(1)} collective-permute-done((bf16[28,384]{1,0:T(8,128)(2,1)S(1)}, bf16[28,384]{1,0:T(8,128)(2,1)S(1)}, u32[]{:S(2)}, u32[]{:S(2)}) %collective-permute-start.7) | collective-permute-done | bytes 21536
  124.9 8.5 %all-to-all-start.2 = ((bf16[32,8,360]{2,1,0:T(8,128)(2,1)}), bf16[32,8,360]{2,1,0:T(8,128)(2,1)S(1)}, u32[]{:S(2)}, u32[]{:S(2)}) async-start(bf16[32,8,360]{2,1,0:T(8,128)(2,1)} %bitcast.37), calls=%async_computation.2 | async-start | bytes 393216 | tf_op jit(solution)/shard_map/all_to_all | solution.py:315
  135.0 7.8 %all-to-all-done.2 = bf16[32,8,360]{2,1,0:T(8,128)(2,1)S(1)} async-done(((bf16[32,8,360]{2,1,0:T(8,128)(2,1)}), bf16[32,8,360]{2,1,0:T(8,128)(2,1)S(1)}, u32[]{:S(2)}, u32[]{:S(2)}) %all-to-all-start.2) | async-done | bytes 184352 | tf_op jit(solution)/shard_map/all_to_all | solution.py:315
  143.6 12.3 %collective-permute-start.6 = (f32[216,256]{1,0:T(8,128)S(1)}, f32[216,256]{1,0:T(8,128)S(1)}, u32[]{:S(2)}, u32[]{:S(2)}) collective-permute-start(f32[216,256]{1,0:T(8,128)S(1)} %get-tuple-element.31), channel_id=1, source_target_pairs={{0,1},{1,0},{2,3},{3,2},{4,5},{5,4},{6,7},{7,6},{8,9},{9,8},{10,11... | collective-permute-start | bytes 663560 | tf_op jit(solution)/shard_map/ppermute | solution.py:283
  (34 shorter events, 13.3 us)
Async XLA Ops:
  0.6 8.9 %copy-start.7 = (bf16[256,180]{0,1:T(8,128)(2,1)S(1)}, bf16[256,180]{0,1:T(8,128)(2,1)}, u32[]{:S(2)}) copy-start(bf16[256,180]{0,1:T(8,128)(2,1)} %param.11) | copy-start | bytes 276484
  0.6 8.9 %copy-start.8 = (bf16[256,180]{0,1:T(8,128)(2,1)S(1)}, bf16[256,180]{0,1:T(8,128)(2,1)}, u32[]{:S(2)}) copy-start(bf16[256,180]{0,1:T(8,128)(2,1)} %param.10) | copy-start | bytes 276484
  6.9 71.5 %collective-permute-start = (bf16[25,184,384]{2,1,0:T(8,128)(2,1)S(1)}, bf16[25,184,384]{2,1,0:T(8,128)(2,1)}, u32[]{:S(2)}, u32[]{:S(2)}) collective-permute-start(bf16[25,184,384]{2,1,0:T(8,128)(2,1)S(1)} %shard_map.121.near), channel_id=1, source_target_pairs={{0,1},{1,0},{2,3},{3,2},{4,5},{5,4},{6,7},{7,6},{8,9},{9,8},{10,11... | collective-permute-start | bytes 10598408 | tf_op jit(solution)/shard_map/ppermute | solution.py:283
  10.3 5.5 %collective-permute-start.1 = (bf16[360,256]{1,0:T(8,128)(2,1)}, bf16[360,256]{1,0:T(8,128)(2,1)}, u32[]{:S(2)}, u32[]{:S(2)}) collective-permute-start(bf16[360,256]{1,0:T(8,128)(2,1)} %pad_maximum_fusion.near), channel_id=1, source_target_pairs={{0,1},{1,0},{2,3},{3,2},{4,5},{5,4},{6,7},{7,6},{8,9},{9,8},{10,11... | collective-permute-start | bytes 552968 | tf_op jit(solution)/shard_map/ppermute | solution.py:283
  40.4 7.6 %copy-start.5 = (bf16[32,8,360]{2,1,0:T(8,128)(2,1)}, bf16[32,8,360]{2,1,0:T(8,128)(2,1)S(1)}, u32[]{:S(2)}) copy-start(bf16[32,8,360]{2,1,0:T(8,128)(2,1)S(1)} %all_to_all.15) | copy-start | bytes 552964
  40.4 7.6 %collective-permute-start.2 = (bf16[256,360]{1,0:T(8,128)(2,1)S(1)}, bf16[256,360]{1,0:T(8,128)(2,1)S(1)}, u32[]{:S(2)}, u32[]{:S(2)}) collective-permute-start(bf16[256,360]{1,0:T(8,128)(2,1)S(1)} %bitcast.38), channel_id=1, source_target_pairs={{0,2},{1,15},{2,0},{3,5},{4,6},{5,3},{6,4},{7,9},{8,10},{9,7},{10,... | collective-permute-start | bytes 552968 | tf_op jit(solution)/shard_map/ppermute | solution.py:291
  48.9 8.5 %collective-permute-start.3 = (bf16[512,360]{1,0:T(8,128)(2,1)S(1)}, bf16[512,360]{1,0:T(8,128)(2,1)S(1)}, u32[]{:S(2)}, u32[]{:S(2)}) collective-permute-start(bf16[512,360]{1,0:T(8,128)(2,1)S(1)} %shard_map.124.first), channel_id=1, source_target_pairs={{0,14},{1,3},{2,4},{3,1},{4,2},{5,7},{6,8},{7,5},{8,6},{9,11},{10,... | collective-permute-start | bytes 1105928 | tf_op jit(solution)/shard_map/ppermute | solution.py:291
  50.9 0.7 copy-start
  57.5 0.8 copy-start.6
  58.2 9.8 %collective-permute-start.4 = (bf16[512,360]{1,0:T(8,128)(2,1)S(1)}, bf16[512,360]{1,0:T(8,128)(2,1)}, u32[]{:S(2)}, u32[]{:S(2)}) collective-permute-start(bf16[512,360]{1,0:T(8,128)(2,1)S(1)} %collective-permute-done.3.second), channel_id=1, source_target_pairs={{0,2},{1,15},{2,0},{3,5},{4,6},{5,3},{6,4},{7,9},{8,10},{9,7},{10,... | collective-permute-start | bytes 1105928 | tf_op jit(solution)/shard_map/ppermute | solution.py:291
  68.1 19.9 %collective-permute-start.5 = (bf16[512,360]{1,0:T(8,128)(2,1)}, bf16[512,360]{1,0:T(8,128)(2,1)}, u32[]{:S(2)}, u32[]{:S(2)}) collective-permute-start(bf16[512,360]{1,0:T(8,128)(2,1)} %collective-permute-done.4.third), channel_id=1, source_target_pairs={{0,14},{1,3},{2,4},{3,1},{4,2},{5,7},{6,8},{7,5},{8,6},{9,11},{10,... | collective-permute-start | bytes 1105928 | tf_op jit(solution)/shard_map/ppermute | solution.py:291
  72.5 15.4 %all-to-all-start.1 = ((bf16[32,8,360]{2,1,0:T(8,128)(2,1)}), bf16[32,8,360]{2,1,0:T(8,128)(2,1)}, u32[]{:S(2)}, u32[]{:S(2)}) async-start(bf16[32,8,360]{2,1,0:T(8,128)(2,1)} %bitcast.36), calls=%async_computation.1 | async-start | bytes 393216 | tf_op jit(solution)/shard_map/all_to_all | solution.py:315
  78.4 1.0 copy-start.1
  93.9 29.9 %copy-start.4 = (bf16[16,360]{1,0:T(8,128)(2,1)S(1)}, bf16[16,360]{1,0:T(8,128)(2,1)}, u32[]{:S(2)}) copy-start(bf16[16,360]{1,0:T(8,128)(2,1)} %get-tuple-element.24.up) | copy-start | bytes 34564
  116.5 26.3 %copy-start.2 = (bf16[256,256]{1,0:T(8,128)(2,1)S(1)}, bf16[256,256]{1,0:T(8,128)(2,1)}, u32[]{:S(2)}) copy-start(bf16[256,256]{1,0:T(8,128)(2,1)} %get-tuple-element.21.pick) | copy-start | bytes 393220
  116.5 26.3 %copy-start.3 = (bf16[256,256]{1,0:T(8,128)(2,1)S(1)}, bf16[256,256]{1,0:T(8,128)(2,1)}, u32[]{:S(2)}) copy-start(bf16[256,256]{1,0:T(8,128)(2,1)} %get-tuple-element.22.weigh) | copy-start | bytes 393220
  116.5 6.5 %collective-permute-start.7 = (bf16[28,384]{1,0:T(8,128)(2,1)S(1)}, bf16[28,384]{1,0:T(8,128)(2,1)S(1)}, u32[]{:S(2)}, u32[]{:S(2)}) collective-permute-start(bf16[28,384]{1,0:T(8,128)(2,1)S(1)} %slice), channel_id=1, source_target_pairs={{0,2},{2,4},{4,6},{6,8},{8,10},{10,12},{12,14},{1,3},{3,5},{5,7},{... | collective-permute-start | bytes 64520
  124.9 17.9 %all-to-all-start.2 = ((bf16[32,8,360]{2,1,0:T(8,128)(2,1)}), bf16[32,8,360]{2,1,0:T(8,128)(2,1)S(1)}, u32[]{:S(2)}, u32[]{:S(2)}) async-start(bf16[32,8,360]{2,1,0:T(8,128)(2,1)} %bitcast.37), calls=%async_computation.2 | async-start | bytes 393216 | tf_op jit(solution)/shard_map/all_to_all | solution.py:315
  143.6 13.4 %collective-permute-start.6 = (f32[216,256]{1,0:T(8,128)S(1)}, f32[216,256]{1,0:T(8,128)S(1)}, u32[]{:S(2)}, u32[]{:S(2)}) collective-permute-start(f32[216,256]{1,0:T(8,128)S(1)} %get-tuple-element.31), channel_id=1, source_target_pairs={{0,1},{1,0},{2,3},{3,2},{4,5},{5,4},{6,7},{7,6},{8,9},{9,8},{10,11... | collective-permute-start | bytes 663560 | tf_op jit(solution)/shard_map/ppermute | solution.py:283

commit v4 on v3

--- a/solution.py
+++ b/solution.py
@@ -145,28 +145,58 @@
     return lax.rem(where[0] + where[2] * ORDER[q] + parts, parts)
 
 
-def project_into(where, first, near, far, blocks, before, sums):
+def pick_call(body, out_shape, where, picked, *args, local=(), scratch=()):
+    near, far, blocks = picked
+    near, far, *args = [
+        pltpu.with_memory_space_constraint(x, pltpu.VMEM if any(x is y for y in local) else pltpu.HBM)
+        for x in (near, far, *args)
+    ]
+    specs = []
+    for _ in range(2):
+        for rows, place in blocks:
+            specs.append(
+                pl.BlockSpec((rows,) + near.shape[1:], lambda i, w, place=place: (place(w), 0, 0))
+            )
+    whole = lambda dims: pl.BlockSpec(dims, lambda i, w, n=len(dims): (0,) * n)
+    return pl.pallas_call(
+        body,
+        out_shape=[pltpu.HBM(dims, kind) for dims, kind in out_shape],
+        grid_spec=pltpu.PrefetchScalarGridSpec(
+            num_scalar_prefetch=1,
+            grid=(1,),
+            in_specs=specs + [whole(x.shape) for x in args],
+            out_specs=[whole(dims) for dims, _ in out_shape],
+            scratch_shapes=list(scratch),
+        ),
+        compiler_params=pltpu.CompilerParams(vmem_limit_bytes=32 << 20),
+    )(where, *([near] * len(blocks)), *([far] * len(blocks)), *args)
+
+
+def project_into(weights, blocks, before, sums):
     hidden, count = sums.shape[3], sums.shape[2]
     piece = blocks[0].shape[1]
     spans = [(x, h * count) for x in blocks for h in range(2)]
-    for n, weights in enumerate((near, far)):
+    for n in range(2):
         for c in range(2):
             acc = jnp.zeros((count, hidden), F32) if before is None else before[n, c]
             for q, (x, at) in enumerate(spans):
-                part = weights[2 * source(where, first + q) + c, :hidden, :piece]
+                part = weights[n * len(spans) + q][c, :hidden, :piece]
                 acc = acc + dot(x[at : at + count, :], part, NT)
             sums[n, c] = acc
 
 
-def project_four(where, near, far, first, second, sums):
-    project_into(where, 0, near, far, (first, second), None, sums)
-
-
-def project_more(where, near, far, third, before, sums):
-    project_into(where, 4, near, far, (third,), before, sums)
-
-
-def expert(where, near, far, sums, last, grads, act_near, act_far, up, out, wide):
+def project_four(where, a, b, c, d, e, f, g, h, first, second, sums):
+    project_into((a, b, c, d, e, f, g, h), (first, second), None, sums)
+
+
+def project_more(where, a, b, c, d, third, before, sums):
+    project_into((a, b, c, d), (third,), before, sums)
+
+
+def expert(
+    where, near_a, near_b, near_down, near_up, far_a, far_b, far_down, far_up,
+    sums, last, grads, act_near, act_far, up, out, wide,
+):
     side = where[1]
     count, hidden = act_near.shape
     piece = last.shape[1]
@@ -176,12 +206,12 @@
     tall = out.shape[0] // parts
     pad = out.shape[1]
     acts = []
-    for n, (weights, act) in enumerate(((near, act_near), (far, act_far))):
+    for n, (weights, act) in enumerate((((near_a, near_b), act_near), ((far_a, far_b), act_far))):
         total = []
         for c in range(2):
             acc = sums[n, c]
             for h in range(2):
-                part = weights[2 * source(where, parts - 2 + h) + c, :hidden, :piece]
+                part = weights[h][c, :hidden, :piece]
                 acc = acc + dot(last[h * count : (h + 1) * count, :], part, NT)
             total.append(acc)
         gate = jnp.minimum(total[0], CLAMP_LIMIT)
@@ -192,7 +222,7 @@
     row, col = iota((half, piece), 0), iota((half, piece), 1)
     here = jnp.where(row + side * half == col, 1.0, 0.0).astype(BF)
     there = jnp.where(row + (1 - side) * half == col, 1.0, 0.0).astype(BF)
-    both = dot(near[3 * parts, :rank, :half], here, NN) + dot(far[3 * parts, :rank, :half], there, NN)
+    both = dot(near_up[0, :rank, :half], here, NN) + dot(far_up[0, :rank, :half], there, NN)
     both = both.astype(BF)
     up[...] = both
     few = rank // 2
@@ -203,7 +233,7 @@
     beside = dot(grads[...], dot(spread.astype(BF), both, NN).astype(BF), NT)
     back = dot(both, grads[...], NT)[:few]
     for a in range(parts):
-        total = dot(acts[0], near[2 * parts + a, :hidden, :], NN) + dot(acts[1], far[2 * parts + a, :hidden, :], NN)
+        total = dot(acts[0], near_down[a, :hidden, :], NN) + dot(acts[1], far_down[a, :hidden, :], NN)
         wide[a * tall : a * tall + count, :] = total + beside
         wide[a * tall + count : (a + 1) * tall, :] = jnp.zeros((tall - count, pad), F32)
         wide[a * tall + count : a * tall + count + few, :count] = back
@@ -326,27 +356,35 @@
         down_block_scales[0][:, None, :],
         adapter_down_matrix[0].T,
         adapter_up_matrix[0],
-        scalars=0, keep=True,
+        scalars=0,
     )
     far = swap(near)
 
     x1 = trade_along(x0, 1)
-    (first,) = call(join, [((2 * slots, piece), BF)], x0, x1, scalars=0, keep=True, local=(1,))
+    (first,) = call(join, [((2 * slots, piece), BF)], x0, x1, scalars=0, keep=True, local=(0, 1))
     second = trade_along(first, -1)
     third = trade_along(second, 1)
     last = trade_along(third, -1)
-    (sums,) = call(
-        project_four, [((2, 2, slots, hidden), F32)], where, near, far, first, second, local=(1, 2, 3)
-    )
-    (sums,) = call(
-        project_more, [((2, 2, slots, hidden), F32)], where, near, far, third, sums, local=(1, 2)
+
+    def arriving(begin, end):
+        return [(2, lambda w, q=q: source(w, q)) for q in range(begin, end)]
+
+    (sums,) = pick_call(
+        project_four, [((2, 2, slots, hidden), F32)],
+        where, (near, far, arriving(0, 4)), first, second, local=(first, second),
+    )
+    (sums,) = pick_call(
+        project_more, [((2, 2, slots, hidden), F32)],
+        where, (near, far, arriving(4, 6)), third, sums, local=(third,),
     )
     tall = slots + rank // 2 + 4
-    act_near, act_far, up, partial = call(
+    act_near, act_far, up, partial = pick_call(
         expert,
         [((slots, hidden), BF)] * 2 + [((rank, piece), BF), ((ring * tall, pad), BF)],
-        where, near, far, sums, last, got_grads,
-        local=(1, 2, 4),
+        where,
+        (near, far, arriving(6, 8) + [(ring, lambda w: 2), (1, lambda w: 3 * ring)]),
+        sums, last, got_grads,
+        local=(last, got_grads),
         scratch=[pltpu.VMEM((ring * tall, pad), F32)],
     )
     groups = [[2 * y + c for y in range(ring)] for c in range(2)]
@@ -359,7 +397,7 @@
         gradients,
         [((rank, hidden), F32), ((rank, width), F32), ((2 * rank, count), F32)],
         where, total, act_near, act_far, got_grads,
-        keep=True, local=(1,),
+        keep=True, local=(1,), free=(2, 3, 4),
     )
     mine, send = call(
         combine,

time: 158 us -> 157 us (level)
  local copies, waits for them, and re-layouts: 4.66 us -> 2.18 us
  waiting for transfers between devices: 32.2 us -> 34.6 us
    pallas_call x0 -> x3, Pallas kernels: none -> 14.8 us  [pick_call(): pl.pallas_call(body, out_shape=[pltpu.HBM(dims, kind) for dims, kind in o...]
    pallas_call x12 -> x9, Pallas kernels: 32.6 us -> 17.9 us  [call(): pl.pallas_call(body, out_shape=[(pltpu.VMEM if keep is True or i in keep...]
    unnamed x22, local copies, waits for them, and re-layouts: 4.66 us -> 2.18 us
  transfers between devices with their start and end apart: 10 -> 10, of which waited for: 7 -> 8; matrix products, arithmetic and copies ran while one was open for 1% -> 1% of each run, Pallas kernels for 11% -> 10%
where the time goes in v4:
time: 157 us; the launch traced here: 156 us
  blocking collectives  45.1 us (29%)
  starting transfers between devices  39.7 us (25%)
  waiting for transfers between devices  34.6 us (22%)
  Pallas kernels  32.8 us (21%)
  local copies, waits for them, and re-layouts  2.18 us (1%)
  between operations  1.57 us (1%)
    unnamed x1, blocking collectives  22.8 us
    all_to_all x1, blocking collectives, trade(): lax.all_to_all(x, 'ctx', split_axis=0, concat_axis=0, tiled=True)  22.3 us
    ppermute x4, waiting for transfers between devices, trade_along(): return lax.ppermute(x, 'exp', pairs)  19.8 us
    pallas_call x9, Pallas kernels, call(): pl.pallas_call(body, out_shape=[(pltpu.VMEM if keep is True or i in keep...  17.9 us
    ppermute x3, starting transfers between devices, swap(): return lax.ppermute(x, 'exp', swap_pairs)  16.2 us
    pallas_call x3, Pallas kernels, pick_call(): pl.pallas_call(body, out_shape=[pltpu.HBM(dims, kind) for dims, kind in o...  14.8 us
    all_to_all x2, starting transfers between devices, trade(): lax.all_to_all(x, 'ctx', split_axis=0, concat_axis=0, tiled=True)  13.5 us
    all_to_all x2, waiting for transfers between devices, trade(): lax.all_to_all(x, 'ctx', split_axis=0, concat_axis=0, tiled=True)  9.36 us
  transfers between devices with their start and end apart: 10, of which 8 were waited for; matrix products, arithmetic and copies ran while one was open for 1% of the time, Pallas kernels for 10%

profile of v4, /device:TPU:33, one launch (start us, length us, event | category | flops | bytes accessed | tf_op | source)
XLA Modules:
  0.0 156.0 jit_solution(9149642498679299607)
XLA Ops:
  0.7 8.0 %shard_map.121.a.b.c.d.near_a.near_b.near_down.near_up = bf16[25,184,384]{2,1,0:T(8,128)(2,1)} custom-call(bf16[180,2,2880]{2,1,0:T(2,128)(2,1)} %bitcast.38, f32[180,2,90]{2,1,0:T(2,128)} %bitcast.43, bf16[180,2880]{1,0:T(8,128)(2,1)} %bitcast.39, f32[180,1,90]{2,1,0:T(1,128)} %bitcast.46, bf16[16,180]{1,0:T(8,128)(2,1)} %bitcast.47, bf16[16,180]{1,0:T(8,128)(2,1)} %bitcast.48), custom_call_target="tpu_custom_call" | custom-call | tf_op jit(solution)/shard_map/pallas_call | solution.py:50
  8.7 2.6 %collective-permute-start = (bf16[25,184,384]{2,1,0:T(8,128)(2,1)}, bf16[25,184,384]{2,1,0:T(8,128)(2,1)}, u32[]{:S(2)}, u32[]{:S(2)}) collective-permute-start(bf16[25,184,384]{2,1,0:T(8,128)(2,1)} %shard_map.121.a.b.c.d.near_a.near_b.near_down.near_up), channel_id=1, source_target_pairs={{0,1},{1,0},{2,3},{3,2},{4,5},{5,4},{6,7},{7,6},{8,9},{9,8},{10,11... | collective-permute-start | bytes 10598408 | tf_op jit(solution)/shard_map/ppermute | solution.py:313
  11.3 1.9 %collective-permute-start.1 = (bf16[360,256]{1,0:T(8,128)(2,1)S(1)}, bf16[360,256]{1,0:T(8,128)(2,1)S(1)}, u32[]{:S(2)}, u32[]{:S(2)}) collective-permute-start(bf16[360,256]{1,0:T(8,128)(2,1)S(1)} %pad_maximum_fusion.near), channel_id=1, source_target_pairs={{0,1},{1,0},{2,3},{3,2},{4,5},{5,4},{6,7},{7,6},{8,9},{9,8},{10,11... | collective-permute-start | bytes 552968 | tf_op jit(solution)/shard_map/ppermute | solution.py:313
  15.1 2.4 %collective-permute-done.1.far = bf16[360,256]{1,0:T(8,128)(2,1)S(1)} collective-permute-done((bf16[360,256]{1,0:T(8,128)(2,1)S(1)}, bf16[360,256]{1,0:T(8,128)(2,1)S(1)}, u32[]{:S(2)}, u32[]{:S(2)}) %collective-permute-start.1) | collective-permute-done | bytes 184352 | tf_op jit(solution)/shard_map/ppermute | solution.py:313
  17.6 1.9 %shard_map.123 = bf16[256,360]{1,0:T(8,128)(2,1)} custom-call(s32[3]{0:T(128)S(1)} %pad_add_fusion.where, bf16[256,256]{1,0:T(8,128)(2,1)S(1)} %get-tuple-element.19.one, bf16[360,256]{1,0:T(8,128)(2,1)S(1)} %pad_maximum_fusion.near, bf16[360,256]{1,0:T(8,128)(2,1)S(1)} %collective-permute-done.1.far), custom_call_target="tpu_custom_call" | custom-call | tf_op jit(solution)/shard_map/pallas_call | solution.py:50
  19.5 22.3 %all_to_all.15 = bf16[32,8,360]{2,1,0:T(8,128)(2,1)S(1)} all-to-all(bf16[32,8,360]{2,1,0:T(8,128)(2,1)} %bitcast.42), channel_id=1, replica_groups=mesh['ctx'=32,'exp'=16] {'ctx'}, dimensions={0} | all-to-all | bytes 368640 | tf_op jit(solution)/shard_map/all_to_all | solution.py:345
  41.8 2.1 %collective-permute-start.2 = (bf16[256,360]{1,0:T(8,128)(2,1)S(1)}, bf16[256,360]{1,0:T(8,128)(2,1)S(1)}, u32[]{:S(2)}, u32[]{:S(2)}) collective-permute-start(bf16[256,360]{1,0:T(8,128)(2,1)S(1)} %bitcast.36), channel_id=1, source_target_pairs={{0,2},{1,15},{2,0},{3,5},{4,6},{5,3},{6,4},{7,9},{8,10},{9,7},{10,... | collective-permute-start | bytes 552968 | tf_op jit(solution)/shard_map/ppermute | solution.py:321
  43.8 5.5 %collective-permute-done.2.second = bf16[256,360]{1,0:T(8,128)(2,1)S(1)} collective-permute-done((bf16[256,360]{1,0:T(8,128)(2,1)S(1)}, bf16[256,360]{1,0:T(8,128)(2,1)S(1)}, u32[]{:S(2)}, u32[]{:S(2)}) %collective-permute-start.2) | collective-permute-done | bytes 184352 | tf_op jit(solution)/shard_map/ppermute | solution.py:321
  49.4 1.9 %collective-permute-start.3 = (bf16[512,360]{1,0:T(8,128)(2,1)S(1)}, bf16[512,360]{1,0:T(8,128)(2,1)S(1)}, u32[]{:S(2)}, u32[]{:S(2)}) collective-permute-start(bf16[512,360]{1,0:T(8,128)(2,1)S(1)} %shard_map.124.first), channel_id=1, source_target_pairs={{0,14},{1,3},{2,4},{3,1},{4,2},{5,7},{6,8},{7,5},{8,6},{9,11},{10,... | collective-permute-start | bytes 1105928 | tf_op jit(solution)/shard_map/ppermute | solution.py:321
  51.3 6.6 %collective-permute-done.3.second = bf16[512,360]{1,0:T(8,128)(2,1)S(1)} collective-permute-done((bf16[512,360]{1,0:T(8,128)(2,1)S(1)}, bf16[512,360]{1,0:T(8,128)(2,1)S(1)}, u32[]{:S(2)}, u32[]{:S(2)}) %collective-permute-start.3) | collective-permute-done | bytes 368672 | tf_op jit(solution)/shard_map/ppermute | solution.py:321
  57.9 2.1 %collective-permute-start.4 = (bf16[512,360]{1,0:T(8,128)(2,1)S(1)}, bf16[512,360]{1,0:T(8,128)(2,1)S(1)}, u32[]{:S(2)}, u32[]{:S(2)}) collective-permute-start(bf16[512,360]{1,0:T(8,128)(2,1)S(1)} %collective-permute-done.3.second), channel_id=1, source_target_pairs={{0,2},{1,15},{2,0},{3,5},{4,6},{5,3},{6,4},{7,9},{8,10},{9,7},{10,... | collective-permute-start | bytes 1105928 | tf_op jit(solution)/shard_map/ppermute | solution.py:321
  60.0 7.6 %collective-permute-done.4.third = bf16[512,360]{1,0:T(8,128)(2,1)S(1)} collective-permute-done((bf16[512,360]{1,0:T(8,128)(2,1)S(1)}, bf16[512,360]{1,0:T(8,128)(2,1)S(1)}, u32[]{:S(2)}, u32[]{:S(2)}) %collective-permute-start.4) | collective-permute-done | bytes 368672 | tf_op jit(solution)/shard_map/ppermute | solution.py:321
  67.7 1.9 %collective-permute-start.5 = (bf16[512,360]{1,0:T(8,128)(2,1)S(1)}, bf16[512,360]{1,0:T(8,128)(2,1)S(1)}, u32[]{:S(2)}, u32[]{:S(2)}) collective-permute-start(bf16[512,360]{1,0:T(8,128)(2,1)S(1)} %collective-permute-done.4.third), channel_id=1, source_target_pairs={{0,14},{1,3},{2,4},{3,1},{4,2},{5,7},{6,8},{7,5},{8,6},{9,11},{10,... | collective-permute-start | bytes 1105928 | tf_op jit(solution)/shard_map/ppermute | solution.py:321
  69.6 2.5 %shard_map.127 = bf16[256,360]{1,0:T(8,128)(2,1)} custom-call(s32[3]{0:T(128)S(1)} %pad_add_fusion.where, bf16[256,256]{1,0:T(8,128)(2,1)} %get-tuple-element.20.one, bf16[256,256]{1,0:T(8,128)(2,1)} %get-tuple-element.21.pick, bf16[256,256]{1,0:T(8,128)(2,1)} %get-tuple-element.22.weigh, bf16[360,256]{1,0:T(8,128)(2,1)} %copy-done, bf16[360,256]{1,0:T(8,128)(2,1)} %copy-done.1), custom_call_target="tpu_custom_call" | custom-call | tf_op jit(solution)/shard_map/pallas_call | solution.py:50
  72.1 5.8 %all-to-all-start.1 = ((bf16[32,8,360]{2,1,0:T(8,128)(2,1)}), bf16[32,8,360]{2,1,0:T(8,128)(2,1)S(1)}, u32[]{:S(2)}, u32[]{:S(2)}) async-start(bf16[32,8,360]{2,1,0:T(8,128)(2,1)} %bitcast.40), calls=%async_computation.1 | async-start | bytes 393216 | tf_op jit(solution)/shard_map/all_to_all | solution.py:345
  77.9 4.4 %shard_map.125.before = f32[2,2,256,180]{3,2,1,0:T(8,128)} custom-call(s32[3]{0:T(128)S(1)} %pad_add_fusion.where, bf16[25,184,384]{2,1,0:T(8,128)(2,1)} %shard_map.121.a.b.c.d.near_a.near_b.near_down.near_up, bf16[25,184,384]{2,1,0:T(8,128)(2,1)} %shard_map.121.a.b.c.d.near_a.near_b.near_down.near_up, ...), custom_call_target="tpu_custom_call" | custom-call | tf_op jit(solution)/shard_map/pallas_call | solution.py:161
  82.3 3.9 %shard_map.126.sums = f32[2,2,256,180]{3,2,1,0:T(8,128)} custom-call(s32[3]{0:T(128)S(1)} %pad_add_fusion.where, bf16[25,184,384]{2,1,0:T(8,128)(2,1)} %shard_map.121.a.b.c.d.near_a.near_b.near_down.near_up, bf16[25,184,384]{2,1,0:T(8,128)(2,1)} %shard_map.121.a.b.c.d.near_a.near_b.near_down.near_up, ...), custom_call_target="tpu_custom_call" | custom-call | tf_op jit(solution)/shard_map/pallas_call | solution.py:161
  87.3 6.5 %shard_map.128 = (bf16[256,180]{1,0:T(8,128)(2,1)}, bf16[256,180]{1,0:T(8,128)(2,1)}, bf16[16,360]{1,0:T(8,128)(2,1)}, bf16[2144,384]{1,0:T(8,128)(2,1)}) custom-call(s32[3]{0:T(128)S(1)} %pad_add_fusion.where, bf16[25,184,384]{2,1,0:T(8,128)(2,1)} %shard_map.121.a.b.c.d.near_a.near_b.near_down.near_up, ...), custom_call_target="tpu_custom_call" | custom-call | tf_op jit(solution)/shard_map/pallas_call | solution.py:161
  93.8 22.8 %fusion = bf16[272,384]{1,0:T(8,128)(2,1)S(1)} fusion(bf16[2144,384]{1,0:T(8,128)(2,1)} %get-tuple-element.23), kind=kCustom, calls=%all-reduce-scatter | all-reduce-scatter fusion | flops 835585 | bytes 1857536
  116.7 2.1 %collective-permute-start.7 = (bf16[28,384]{1,0:T(8,128)(2,1)S(1)}, bf16[28,384]{1,0:T(8,128)(2,1)S(1)}, u32[]{:S(2)}, u32[]{:S(2)}) collective-permute-start(bf16[28,384]{1,0:T(8,128)(2,1)S(1)} %slice), channel_id=1, source_target_pairs={{0,2},{2,4},{4,6},{6,8},{8,10},{10,12},{12,14},{1,3},{3,5},{5,7},{... | collective-permute-start | bytes 64520
  120.7 1.9 %collective-permute-done.7 = bf16[28,384]{1,0:T(8,128)(2,1)S(1)} collective-permute-done((bf16[28,384]{1,0:T(8,128)(2,1)S(1)}, bf16[28,384]{1,0:T(8,128)(2,1)S(1)}, u32[]{:S(2)}, u32[]{:S(2)}) %collective-permute-start.7) | collective-permute-done | bytes 21536
  124.5 7.7 %all-to-all-start.2 = ((bf16[32,8,360]{2,1,0:T(8,128)(2,1)}), bf16[32,8,360]{2,1,0:T(8,128)(2,1)S(1)}, u32[]{:S(2)}, u32[]{:S(2)}) async-start(bf16[32,8,360]{2,1,0:T(8,128)(2,1)} %bitcast.41), calls=%async_computation.2 | async-start | bytes 393216 | tf_op jit(solution)/shard_map/all_to_all | solution.py:345
  133.3 8.3 %all-to-all-done.2 = bf16[32,8,360]{2,1,0:T(8,128)(2,1)S(1)} async-done(((bf16[32,8,360]{2,1,0:T(8,128)(2,1)}), bf16[32,8,360]{2,1,0:T(8,128)(2,1)S(1)}, u32[]{:S(2)}, u32[]{:S(2)}) %all-to-all-start.2) | async-done | bytes 184352 | tf_op jit(solution)/shard_map/all_to_all | solution.py:345
  142.5 11.7 %collective-permute-start.6 = (f32[216,256]{1,0:T(8,128)S(1)}, f32[216,256]{1,0:T(8,128)S(1)}, u32[]{:S(2)}, u32[]{:S(2)}) collective-permute-start(f32[216,256]{1,0:T(8,128)S(1)} %get-tuple-element.31), channel_id=1, source_target_pairs={{0,1},{1,0},{2,3},{3,2},{4,5},{5,4},{6,7},{7,6},{8,9},{9,8},{10,11... | collective-permute-start | bytes 663560 | tf_op jit(solution)/shard_map/ppermute | solution.py:313
  (34 shorter events, 9.9 us)
Async XLA Ops:
  0.6 10.6 %copy-start.7 = (bf16[256,180]{0,1:T(8,128)(2,1)S(1)}, bf16[256,180]{0,1:T(8,128)(2,1)}, u32[]{:S(2)}) copy-start(bf16[256,180]{0,1:T(8,128)(2,1)} %param.11) | copy-start | bytes 276484
  0.6 10.6 %copy-start.8 = (bf16[256,180]{0,1:T(8,128)(2,1)S(1)}, bf16[256,180]{0,1:T(8,128)(2,1)}, u32[]{:S(2)}) copy-start(bf16[256,180]{0,1:T(8,128)(2,1)} %param.10) | copy-start | bytes 276484
  8.7 69.2 %collective-permute-start = (bf16[25,184,384]{2,1,0:T(8,128)(2,1)}, bf16[25,184,384]{2,1,0:T(8,128)(2,1)}, u32[]{:S(2)}, u32[]{:S(2)}) collective-permute-start(bf16[25,184,384]{2,1,0:T(8,128)(2,1)} %shard_map.121.a.b.c.d.near_a.near_b.near_down.near_up), channel_id=1, source_target_pairs={{0,1},{1,0},{2,3},{3,2},{4,5},{5,4},{6,7},{7,6},{8,9},{9,8},{10,11... | collective-permute-start | bytes 10598408 | tf_op jit(solution)/shard_map/ppermute | solution.py:313
  11.3 58.2 %copy-start = (bf16[360,256]{1,0:T(8,128)(2,1)}, bf16[360,256]{1,0:T(8,128)(2,1)S(1)}, u32[]{:S(2)}) copy-start(bf16[360,256]{1,0:T(8,128)(2,1)S(1)} %pad_maximum_fusion.near) | copy-start | bytes 552964
  11.3 6.2 %collective-permute-start.1 = (bf16[360,256]{1,0:T(8,128)(2,1)S(1)}, bf16[360,256]{1,0:T(8,128)(2,1)S(1)}, u32[]{:S(2)}, u32[]{:S(2)}) collective-permute-start(bf16[360,256]{1,0:T(8,128)(2,1)S(1)} %pad_maximum_fusion.near), channel_id=1, source_target_pairs={{0,1},{1,0},{2,3},{3,2},{4,5},{5,4},{6,7},{7,6},{8,9},{9,8},{10,11... | collective-permute-start | bytes 552968 | tf_op jit(solution)/shard_map/ppermute | solution.py:313
  17.6 52.0 %copy-start.1 = (bf16[360,256]{1,0:T(8,128)(2,1)}, bf16[360,256]{1,0:T(8,128)(2,1)S(1)}, u32[]{:S(2)}) copy-start(bf16[360,256]{1,0:T(8,128)(2,1)S(1)} %collective-permute-done.1.far) | copy-start | bytes 552964
  41.8 7.6 %collective-permute-start.2 = (bf16[256,360]{1,0:T(8,128)(2,1)S(1)}, bf16[256,360]{1,0:T(8,128)(2,1)S(1)}, u32[]{:S(2)}, u32[]{:S(2)}) collective-permute-start(bf16[256,360]{1,0:T(8,128)(2,1)S(1)} %bitcast.36), channel_id=1, source_target_pairs={{0,2},{1,15},{2,0},{3,5},{4,6},{5,3},{6,4},{7,9},{8,10},{9,7},{10,... | collective-permute-start | bytes 552968 | tf_op jit(solution)/shard_map/ppermute | solution.py:321
  49.4 8.5 %collective-permute-start.3 = (bf16[512,360]{1,0:T(8,128)(2,1)S(1)}, bf16[512,360]{1,0:T(8,128)(2,1)S(1)}, u32[]{:S(2)}, u32[]{:S(2)}) collective-permute-start(bf16[512,360]{1,0:T(8,128)(2,1)S(1)} %shard_map.124.first), channel_id=1, source_target_pairs={{0,14},{1,3},{2,4},{3,1},{4,2},{5,7},{6,8},{7,5},{8,6},{9,11},{10,... | collective-permute-start | bytes 1105928 | tf_op jit(solution)/shard_map/ppermute | solution.py:321
  57.9 9.7 %collective-permute-start.4 = (bf16[512,360]{1,0:T(8,128)(2,1)S(1)}, bf16[512,360]{1,0:T(8,128)(2,1)S(1)}, u32[]{:S(2)}, u32[]{:S(2)}) collective-permute-start(bf16[512,360]{1,0:T(8,128)(2,1)S(1)} %collective-permute-done.3.second), channel_id=1, source_target_pairs={{0,2},{1,15},{2,0},{3,5},{4,6},{5,3},{6,4},{7,9},{8,10},{9,7},{10,... | collective-permute-start | bytes 1105928 | tf_op jit(solution)/shard_map/ppermute | solution.py:321
  67.7 19.7 %collective-permute-start.5 = (bf16[512,360]{1,0:T(8,128)(2,1)S(1)}, bf16[512,360]{1,0:T(8,128)(2,1)S(1)}, u32[]{:S(2)}, u32[]{:S(2)}) collective-permute-start(bf16[512,360]{1,0:T(8,128)(2,1)S(1)} %collective-permute-done.4.third), channel_id=1, source_target_pairs={{0,14},{1,3},{2,4},{3,1},{4,2},{5,7},{6,8},{7,5},{8,6},{9,11},{10,... | collective-permute-start | bytes 1105928 | tf_op jit(solution)/shard_map/ppermute | solution.py:321
  72.1 15.2 %all-to-all-start.1 = ((bf16[32,8,360]{2,1,0:T(8,128)(2,1)}), bf16[32,8,360]{2,1,0:T(8,128)(2,1)S(1)}, u32[]{:S(2)}, u32[]{:S(2)}) async-start(bf16[32,8,360]{2,1,0:T(8,128)(2,1)} %bitcast.40), calls=%async_computation.1 | async-start | bytes 393216 | tf_op jit(solution)/shard_map/all_to_all | solution.py:345
  93.8 29.7 %copy-start.6 = (bf16[16,360]{1,0:T(8,128)(2,1)S(1)}, bf16[16,360]{1,0:T(8,128)(2,1)}, u32[]{:S(2)}) copy-start(bf16[16,360]{1,0:T(8,128)(2,1)} %get-tuple-element.24.up) | copy-start | bytes 34564
  93.8 38.5 %copy-start.4 = (bf16[256,180]{1,0:T(8,128)(2,1)S(1)}, bf16[256,180]{1,0:T(8,128)(2,1)}, u32[]{:S(2)}) copy-start(bf16[256,180]{1,0:T(8,128)(2,1)} %get-tuple-element.25.act_near) | copy-start | bytes 276484
  93.8 38.5 %copy-start.5 = (bf16[256,180]{1,0:T(8,128)(2,1)S(1)}, bf16[256,180]{1,0:T(8,128)(2,1)}, u32[]{:S(2)}) copy-start(bf16[256,180]{1,0:T(8,128)(2,1)} %get-tuple-element.26.act_far) | copy-start | bytes 276484
  116.6 25.0 %copy-start.2 = (bf16[256,256]{1,0:T(8,128)(2,1)S(1)}, bf16[256,256]{1,0:T(8,128)(2,1)}, u32[]{:S(2)}) copy-start(bf16[256,256]{1,0:T(8,128)(2,1)} %get-tuple-element.21.pick) | copy-start | bytes 393220
  116.7 25.0 %copy-start.3 = (bf16[256,256]{1,0:T(8,128)(2,1)S(1)}, bf16[256,256]{1,0:T(8,128)(2,1)}, u32[]{:S(2)}) copy-start(bf16[256,256]{1,0:T(8,128)(2,1)} %get-tuple-element.22.weigh) | copy-start | bytes 393220
  116.7 5.9 %collective-permute-start.7 = (bf16[28,384]{1,0:T(8,128)(2,1)S(1)}, bf16[28,384]{1,0:T(8,128)(2,1)S(1)}, u32[]{:S(2)}, u32[]{:S(2)}) collective-permute-start(bf16[28,384]{1,0:T(8,128)(2,1)S(1)} %slice), channel_id=1, source_target_pairs={{0,2},{2,4},{4,6},{6,8},{8,10},{10,12},{12,14},{1,3},{3,5},{5,7},{... | collective-permute-start | bytes 64520
  124.5 17.1 %all-to-all-start.2 = ((bf16[32,8,360]{2,1,0:T(8,128)(2,1)}), bf16[32,8,360]{2,1,0:T(8,128)(2,1)S(1)}, u32[]{:S(2)}, u32[]{:S(2)}) async-start(bf16[32,8,360]{2,1,0:T(8,128)(2,1)} %bitcast.41), calls=%async_computation.2 | async-start | bytes 393216 | tf_op jit(solution)/shard_map/all_to_all | solution.py:345
  142.5 12.8 %collective-permute-start.6 = (f32[216,256]{1,0:T(8,128)S(1)}, f32[216,256]{1,0:T(8,128)S(1)}, u32[]{:S(2)}, u32[]{:S(2)}) collective-permute-start(f32[216,256]{1,0:T(8,128)S(1)} %get-tuple-element.31), channel_id=1, source_target_pairs={{0,1},{1,0},{2,3},{3,2},{4,5},{5,4},{6,7},{7,6},{8,9},{9,8},{10,11... | collective-permute-start | bytes 663560 | tf_op jit(solution)/shard_map/ppermute | solution.py:313
